TPU v7x, 32 devices: a whole 2x2x4 slice. The times are simulated.
32 devices in a mesh: fsdp: 8 (over y, x, core), seq: 4 (over z).
Axes of the slice: x: 2, y: 2, z: 4, core: 2. Of those that a mesh axis runs over, the one named last changes fastest.
Arguments:
- tokens: bfloat16 [24, 584, 1024], P('fsdp', 'seq'), may hold values from -6 to 6
- counts: int32 [24], P('fsdp'), may hold values from 0 to 577, as said below
- norm1_gain: bfloat16 [1024], P('fsdp'), may hold values from 0.099609375 to 1.8984375
- norm1_shift: bfloat16 [1024], P('fsdp'), may hold values from -3 to 3
- qkv_weight: bfloat16 [1024, 3072], P('fsdp'), may hold values from -0.1875 to 0.1875
- query_bias: bfloat16 [1024], P('fsdp'), may hold values from -3 to 3
- value_bias: bfloat16 [1024], P('fsdp'), may hold values from -3 to 3
- out_weight: bfloat16 [1024, 1024], P('fsdp'), may hold values from -0.875 to 0.875
- out_bias: bfloat16 [1024], P('fsdp'), may hold values from -3 to 3
- norm2_gain: bfloat16 [1024], P('fsdp'), may hold values from 0.099609375 to 1.8984375
- norm2_shift: bfloat16 [1024], P('fsdp'), may hold values from -3 to 3
- fc1_weight: bfloat16 [1024, 4096], P('fsdp'), may hold values from -0.1875 to 0.1875
- fc1_bias: bfloat16 [4096], P('fsdp'), may hold values from -3 to 3
- fc2_weight: bfloat16 [4096, 1024], P('fsdp'), may hold values from -0.09375 to 0.09375
- fc2_bias: bfloat16 [1024], P('fsdp'), may hold values from -3 to 3
- cotangent: bfloat16 [24, 584, 1024], P('fsdp', 'seq'), may hold values from -6 to 6
Outputs:
- output: bfloat16 [24, 584, 1024], P('fsdp', 'seq')
- input_grad: float32 [24, 584, 1024], P('fsdp', 'seq')
- norm1_gain_grad: float32 [1024], P('fsdp')
- norm1_shift_grad: float32 [1024], P('fsdp')
- qkv_weight_grad: float32 [1024, 3072], P('fsdp')
- query_bias_grad: float32 [1024], P('fsdp')
- value_bias_grad: float32 [1024], P('fsdp')
- out_weight_grad: float32 [1024, 1024], P('fsdp')
- out_bias_grad: float32 [1024], P('fsdp')
- norm2_gain_grad: float32 [1024], P('fsdp')
- norm2_shift_grad: float32 [1024], P('fsdp')
- fc1_weight_grad: float32 [1024, 4096], P('fsdp')
- fc1_bias_grad: float32 [4096], P('fsdp')
- fc2_weight_grad: float32 [4096, 1024], P('fsdp')
- fc2_bias_grad: float32 [1024], P('fsdp')
Inputs may be any that keep to these rules, and one draw needn't show every extreme that they name: `counts`: each image's count is 577 or 0; image 0 has 577 and the last image has 0.
All inputs are finite; a program needn't handle non-finite values.
Results may differ from a plain program's by a relative error of at most 0.012.
Values may be sent and summed in bfloat16 or wider, within the bound.
No kernel may reach another device: no remote copies, remote signals or barrier semaphores. Data moves between devices by JAX's collectives and lax.ppermute only.
A program may use at most 192 MiB of HBM per device.

v0:
```python
import jax
import jax.numpy as jnp
from jax import lax
from jax.sharding import PartitionSpec as P

HEAD_DIM = 64


EPS = 1e-05
MASKED = -1e30


def norm_apply(values, gain_vec, shift_vec):
    average = jnp.mean(values, axis=-1, keepdims=True)
    centered = values - average
    inverse = lax.rsqrt(jnp.mean(centered * centered, axis=-1, keepdims=True) + EPS)
    return centered * inverse * gain_vec + shift_vec


def quick_gelu(values):
    return values * jax.nn.sigmoid(1.702 * values)


def inner_rows(left, right):
    return lax.dot_general(
        left, right, (((0,), (0,)), ((), ())), preferred_element_type=jnp.float32
    )


def times_back(left, right):
    return lax.dot_general(
        left, right, (((1,), (1,)), ((), ())), preferred_element_type=jnp.float32
    )


def collect(shards):
    (
        norm1_gain,
        norm1_shift,
        qkv_weight,
        query_bias,
        value_bias,
        out_weight,
        out_bias,
        norm2_gain,
        norm2_shift,
        fc1_weight,
        fc1_bias,
        fc2_weight,
        fc2_bias,
    ) = shards
    return (
        lax.all_gather(norm1_gain, "fsdp", axis=0, tiled=True),
        lax.all_gather(norm1_shift, "fsdp", axis=0, tiled=True),
        lax.all_gather(qkv_weight, "fsdp", axis=0, tiled=True),
        lax.all_gather(query_bias, "fsdp", axis=0, tiled=True),
        lax.all_gather(value_bias, "fsdp", axis=0, tiled=True),
        lax.all_gather(out_weight, "fsdp", axis=0, tiled=True),
        lax.all_gather(out_bias, "fsdp", axis=0, tiled=True),
        lax.all_gather(norm2_gain, "fsdp", axis=0, tiled=True),
        lax.all_gather(norm2_shift, "fsdp", axis=0, tiled=True),
        lax.all_gather(fc1_weight, "fsdp", axis=0, tiled=True),
        lax.all_gather(fc1_bias, "fsdp", axis=0, tiled=True),
        lax.all_gather(fc2_weight, "fsdp", axis=0, tiled=True),
        lax.all_gather(fc2_bias, "fsdp", axis=0, tiled=True),
    )


def masked_scores(query_img, key_img, length):
    positions, features = query_img.shape
    query_split = query_img.reshape(positions, features // HEAD_DIM, HEAD_DIM)
    key_split = key_img.reshape(positions, features // HEAD_DIM, HEAD_DIM)
    scores = jnp.einsum(
        "shd,thd->hst", query_split, key_split, preferred_element_type=jnp.float32
    ) * HEAD_DIM ** (-0.5)
    allowed = lax.broadcasted_iota(jnp.int32, (1, 1, positions), 2) < length
    return jnp.where(allowed, scores, MASKED)


def attend_one(members):
    query_img, key_img, value_img, length = members
    positions, features = query_img.shape
    scores = masked_scores(query_img, key_img, length)
    highest = jnp.max(scores, axis=-1, keepdims=True)
    exponent = jnp.exp(scores - highest)
    denominator = jnp.sum(exponent, axis=-1, keepdims=True)
    attention = (exponent / denominator).astype(jnp.bfloat16)
    value_split = value_img.reshape(positions, features // HEAD_DIM, HEAD_DIM)
    context = jnp.einsum("hst,thd->shd", attention, value_split, preferred_element_type=jnp.float32)
    return (
        context.reshape(positions, features).astype(jnp.bfloat16),
        highest + jnp.log(denominator),
    )


def attend_back(members):
    query_img, key_img, value_img, grad_img, length, log_total = members
    positions, features = query_img.shape
    factor = HEAD_DIM ** (-0.5)
    attention = jnp.exp(masked_scores(query_img, key_img, length) - log_total)
    query_split = query_img.reshape(positions, features // HEAD_DIM, HEAD_DIM)
    key_split = key_img.reshape(positions, features // HEAD_DIM, HEAD_DIM)
    value_split = value_img.reshape(positions, features // HEAD_DIM, HEAD_DIM)
    grad_split = grad_img.reshape(positions, features // HEAD_DIM, HEAD_DIM)
    grad_attention = jnp.einsum(
        "shd,thd->hst", grad_split, value_split, preferred_element_type=jnp.float32
    )
    value_grad = jnp.einsum(
        "hst,shd->thd",
        attention.astype(jnp.bfloat16),
        grad_split,
        preferred_element_type=jnp.float32,
    )
    center = jnp.sum(grad_attention * attention, axis=-1, keepdims=True)
    score_grad = (attention * (grad_attention - center)).astype(jnp.bfloat16)
    query_grad = (
        jnp.einsum("hst,thd->shd", score_grad, key_split, preferred_element_type=jnp.float32)
        * factor
    )
    key_grad = (
        jnp.einsum("hst,shd->thd", score_grad, query_split, preferred_element_type=jnp.float32)
        * factor
    )
    return (
        query_grad.reshape(positions, features).astype(jnp.bfloat16),
        key_grad.reshape(positions, features).astype(jnp.bfloat16),
        value_grad.reshape(positions, features).astype(jnp.bfloat16),
    )


def forward_pass(weights, tokens_in, counts):
    (
        norm1_gain,
        norm1_shift,
        qkv_weight,
        query_bias,
        value_bias,
        out_weight,
        out_bias,
        norm2_gain,
        norm2_shift,
        fc1_weight,
        fc1_bias,
        fc2_weight,
        fc2_bias,
    ) = weights
    images, local_len, features = tokens_in.shape
    rows_in = tokens_in.reshape(images * local_len, features).astype(jnp.float32)
    normed_one = norm_apply(rows_in, norm1_gain, norm1_shift).astype(jnp.bfloat16)
    projected = jnp.dot(normed_one, qkv_weight, preferred_element_type=jnp.float32)
    query_rows = (
        (projected[:, :features] + query_bias)
        .astype(jnp.bfloat16)
        .reshape(images, local_len, features)
    )
    key_rows = (
        projected[:, features : 2 * features]
        .astype(jnp.bfloat16)
        .reshape(images, local_len, features)
    )
    value_rows = (
        (projected[:, 2 * features :] + value_bias)
        .astype(jnp.bfloat16)
        .reshape(images, local_len, features)
    )
    query_heads, key_heads, value_heads = (
        lax.all_to_all(query_rows, "seq", split_axis=2, concat_axis=1, tiled=True),
        lax.all_to_all(key_rows, "seq", split_axis=2, concat_axis=1, tiled=True),
        lax.all_to_all(value_rows, "seq", split_axis=2, concat_axis=1, tiled=True),
    )
    context, log_total = lax.map(attend_one, (query_heads, key_heads, value_heads, counts))
    context_rows = lax.all_to_all(context, "seq", split_axis=1, concat_axis=2, tiled=True).reshape(
        images * local_len, features
    )
    branch = jnp.dot(context_rows, out_weight, preferred_element_type=jnp.float32) + out_bias
    flags = (counts > 0).astype(jnp.float32)
    flag_rows = jnp.broadcast_to(flags[:, None], (images, local_len)).reshape(images * local_len, 1)
    mixed = rows_in + branch * flag_rows
    normed_two = norm_apply(mixed, norm2_gain, norm2_shift).astype(jnp.bfloat16)
    hidden = jnp.dot(normed_two, fc1_weight, preferred_element_type=jnp.float32) + fc1_bias
    active = quick_gelu(hidden).astype(jnp.bfloat16)
    output_rows = mixed + jnp.dot(active, fc2_weight, preferred_element_type=jnp.float32) + fc2_bias
    return (
        rows_in,
        normed_one,
        query_heads,
        key_heads,
        value_heads,
        log_total,
        context_rows,
        flag_rows,
        mixed,
        normed_two,
        hidden,
        active,
        output_rows,
    )


def on_device(
    tokens,
    counts,
    norm1_gain,
    norm1_shift,
    qkv_weight,
    query_bias,
    value_bias,
    out_weight,
    out_bias,
    norm2_gain,
    norm2_shift,
    fc1_weight,
    fc1_bias,
    fc2_weight,
    fc2_bias,
    cotangent,
):
    images, local_len, features = tokens.shape
    shards = (
        norm1_gain,
        norm1_shift,
        qkv_weight,
        query_bias,
        value_bias,
        out_weight,
        out_bias,
        norm2_gain,
        norm2_shift,
        fc1_weight,
        fc1_bias,
        fc2_weight,
        fc2_bias,
    )
    first = forward_pass(collect(shards), tokens, counts)
    output = first[-1].astype(jnp.bfloat16).reshape(images, local_len, features)
    output, shards = lax.optimization_barrier((output, shards))
    weights = collect(shards)
    kept = forward_pass(weights, tokens, counts)
    (
        rows_in,
        normed_one,
        query_heads,
        key_heads,
        value_heads,
        log_total,
        context_rows,
        flag_rows,
        mixed,
        normed_two,
        hidden,
        active,
        unused_rows,
    ) = kept
    (
        gain_one,
        shift_one,
        qkv_full,
        unused_query,
        unused_value,
        out_full,
        unused_out,
        gain_two,
        shift_two,
        fc1_full,
        unused_fc1,
        fc2_full,
        unused_fc2,
    ) = weights
    grad_out = cotangent.reshape(images * local_len, features)
    grad_out32 = grad_out.astype(jnp.float32)
    fc2_bias_grad = jnp.sum(grad_out32, axis=0)
    fc2_weight_grad = inner_rows(active, grad_out)
    grad_active = times_back(grad_out, fc2_full)
    unused_gelu, gelu_back = jax.vjp(quick_gelu, hidden)
    grad_hidden = gelu_back(grad_active)[0].astype(jnp.bfloat16)
    fc1_bias_grad = jnp.sum(grad_hidden.astype(jnp.float32), axis=0)
    fc1_weight_grad = inner_rows(normed_two, grad_hidden)
    grad_normed_two = times_back(grad_hidden, fc1_full)
    unused_norm_two, norm_two_back = jax.vjp(
        norm_apply, mixed, gain_two.astype(jnp.float32), shift_two.astype(jnp.float32)
    )
    grad_mixed_part, norm2_gain_grad, norm2_shift_grad = norm_two_back(grad_normed_two)
    grad_mixed = grad_out32 + grad_mixed_part
    grad_branch = (grad_mixed * flag_rows).astype(jnp.bfloat16)
    out_bias_grad = jnp.sum(grad_branch.astype(jnp.float32), axis=0)
    out_weight_grad = inner_rows(context_rows, grad_branch)
    grad_context = (
        times_back(grad_branch, out_full).astype(jnp.bfloat16).reshape(images, local_len, features)
    )
    grad_heads = lax.all_to_all(grad_context, "seq", split_axis=2, concat_axis=1, tiled=True)
    query_part, key_part, value_part = lax.map(
        attend_back, (query_heads, key_heads, value_heads, grad_heads, counts, log_total)
    )
    query_grad, key_grad, value_grad = (
        lax.all_to_all(query_part, "seq", split_axis=1, concat_axis=2, tiled=True),
        lax.all_to_all(key_part, "seq", split_axis=1, concat_axis=2, tiled=True),
        lax.all_to_all(value_part, "seq", split_axis=1, concat_axis=2, tiled=True),
    )
    qkv_grad = jnp.concatenate((query_grad, key_grad, value_grad), axis=2).reshape(
        images * local_len, 3 * features
    )
    query_bias_grad = jnp.sum(qkv_grad[:, :features].astype(jnp.float32), axis=0)
    value_bias_grad = jnp.sum(qkv_grad[:, 2 * features :].astype(jnp.float32), axis=0)
    qkv_weight_grad = inner_rows(normed_one, qkv_grad)
    grad_normed_one = times_back(qkv_grad, qkv_full)
    unused_norm_one, norm_one_back = jax.vjp(
        norm_apply, rows_in, gain_one.astype(jnp.float32), shift_one.astype(jnp.float32)
    )
    grad_in_part, norm1_gain_grad, norm1_shift_grad = norm_one_back(grad_normed_one)
    input_grad = (grad_mixed + grad_in_part).reshape(images, local_len, features)
    summed = (
        lax.psum_scatter(norm1_gain_grad, "fsdp", scatter_dimension=0, tiled=True),
        lax.psum_scatter(norm1_shift_grad, "fsdp", scatter_dimension=0, tiled=True),
        lax.psum_scatter(qkv_weight_grad, "fsdp", scatter_dimension=0, tiled=True),
        lax.psum_scatter(query_bias_grad, "fsdp", scatter_dimension=0, tiled=True),
        lax.psum_scatter(value_bias_grad, "fsdp", scatter_dimension=0, tiled=True),
        lax.psum_scatter(out_weight_grad, "fsdp", scatter_dimension=0, tiled=True),
        lax.psum_scatter(out_bias_grad, "fsdp", scatter_dimension=0, tiled=True),
        lax.psum_scatter(norm2_gain_grad, "fsdp", scatter_dimension=0, tiled=True),
        lax.psum_scatter(norm2_shift_grad, "fsdp", scatter_dimension=0, tiled=True),
        lax.psum_scatter(fc1_weight_grad, "fsdp", scatter_dimension=0, tiled=True),
        lax.psum_scatter(fc1_bias_grad, "fsdp", scatter_dimension=0, tiled=True),
        lax.psum_scatter(fc2_weight_grad, "fsdp", scatter_dimension=0, tiled=True),
        lax.psum_scatter(fc2_bias_grad, "fsdp", scatter_dimension=0, tiled=True),
    )
    (
        part_g1,
        part_s1,
        part_qkv,
        part_qb,
        part_vb,
        part_ow,
        part_ob,
        part_g2,
        part_s2,
        part_w1,
        part_b1,
        part_w2,
        part_b2,
    ) = summed
    totals = lax.psum(
        (
            part_g1,
            part_s1,
            part_qkv,
            part_qb,
            part_vb,
            part_ow,
            part_ob,
            part_g2,
            part_s2,
            part_w1,
            part_b1,
            part_w2,
            part_b2,
        ),
        "seq",
    )
    return (
        output,
        input_grad,
        totals[0],
        totals[1],
        totals[2],
        totals[3],
        totals[4],
        totals[5],
        totals[6],
        totals[7],
        totals[8],
        totals[9],
        totals[10],
        totals[11],
        totals[12],
    )


def solution(mesh):
    return jax.shard_map(
        on_device,
        mesh=mesh,
        in_specs=(
            P("fsdp", "seq", None),
            P("fsdp"),
            P("fsdp"),
            P("fsdp"),
            P("fsdp", None),
            P("fsdp"),
            P("fsdp"),
            P("fsdp", None),
            P("fsdp"),
            P("fsdp"),
            P("fsdp"),
            P("fsdp", None),
            P("fsdp"),
            P("fsdp", None),
            P("fsdp"),
            P("fsdp", "seq", None),
        ),
        out_specs=(
            P("fsdp", "seq", None),
            P("fsdp", "seq", None),
            P("fsdp"),
            P("fsdp"),
            P("fsdp", None),
            P("fsdp"),
            P("fsdp"),
            P("fsdp", None),
            P("fsdp"),
            P("fsdp"),
            P("fsdp"),
            P("fsdp", None),
            P("fsdp"),
            P("fsdp", None),
            P("fsdp"),
        ),
        check_vma=False,
    )
```

profile of v0, /device:TPU:0, one launch (start us, length us, event | category | flops | bytes accessed | tf_op | source)
XLA Modules:
  0.0 1322.4 jit_solution(4458114388571986266)
XLA Ops:
  10.3 10.3 all-gather.1
  20.5 9.0 all-gather
  38.3 9.0 all-gather.2
  47.3 10.8 all-gather.26.cloned.1.call-done
  87.4 14.7 %all-to-all-done = bf16[4,2,56064]{2,1,0:T(2,128)(2,1)} async-done(((bf16[4,2,56064]{2,1,0:T(2,128)(2,1)}), bf16[4,2,56064]{2,1,0:T(2,128)(2,1)}, u32[]{:S(2)}, u32[]{:S(2)}) %all-to-all-start) | async-done | bytes 897056 | tf_op jit(solution)/shard_map/all_to_all | solution.py:169
  116.2 12.2 all-to-all-done.1
  165.2 35.4 %while.36 = (s32[]{:T(128)}, bf16[3,584,256]{1,2,0:T(8,128)(2,1)S(1)}, bf16[3,584,256]{1,2,0:T(8,128)(2,1)}, s32[3]{0:T(128)S(1)}, bf16[3,584,256]{1,2,0:T(8,128...) while((s32[]{:T(128)}, bf16[3,584,256]{1,2,0:T(8,128)(2,1)S(1)}, bf16[3,584,256]{1,2,0:T(8,128)(2,1)}, ...), condition=%wide.region_5.6_spmd, body=%wide.region_2.5_spmd.sunk | while | flops 357577344 | bytes 14579201 | solution.py:171
  208.1 8.7 all-gather.4
  242.0 8.6 all-gather.5
  257.3 15.3 %add_convert_fusion.2 = bf16[438,1024]{1,0:T(8,128)(2,1)S(1)} fusion(f32[438,1024]{1,0:T(8,128)} %copy-done.24, bf16[4096,1024]{1,0:T(8,128)(2,1)} %all-gather.32.cloned.1.call-done, f32[1024]{0:T(1024)S(1)} %bitcast.364, bf16[1024,4096]{1,0:T(8,128)(2,1)} %all-gather.30.cloned.1.call-done, f32[4096]{0:T(1024)S(1)} %bitcast.355, f32[1024]{0:T(1024)S(1)} %bitcast.365, ...), kind=kOutput, calls=%fused_computation.98 | convolution fusion | flops 7364567040 | bytes 19500464 | tf_op jit(solution)/shard_map/dot_general | solution.py:182
  283.6 8.5 all-gather.10
  292.0 27.9 %all-gather.36.cloned.1.call-done = bf16[1024,3072]{1,0:T(8,128)(2,1)} async-done(((bf16[128,3072]{1,0:T(8,128)(2,1)}), bf16[1024,3072]{1,0:T(8,128)(2,1)}) %all-gather.36.cloned.1.call-update) | async-done | bytes 6291472 | tf_op jit(solution)/shard_map/all_gather | solution.py:55
  341.5 8.9 all-gather.11
  383.7 14.8 %all-to-all-done.5 = bf16[4,2,56064]{2,1,0:T(2,128)(2,1)} async-done(((bf16[4,2,56064]{2,1,0:T(2,128)(2,1)}), bf16[4,2,56064]{2,1,0:T(2,128)(2,1)}, u32[]{:S(2)}, u32[]{:S(2)}) %all-to-all-start.5) | async-done | bytes 897056 | tf_op jit(solution)/shard_map/all_to_all | solution.py:167
  439.7 20.5 %while.37 = (s32[]{:T(128)}, bf16[3,584,256]{1,2,0:T(8,128)(2,1)}, f32[3,4,584,1]{2,1,3,0:T(4,128)S(1)}, bf16[3,584,256]{1,2,0:T(8,128)(2,1)S(1)}, s32[3]{0:T(12...) while((s32[]{:T(128)}, bf16[3,584,256]{1,2,0:T(8,128)(2,1)}, ...), condition=%wide.region_11.12_spmd, body=%wide.region_8.11_spmd.sunk | while | flops 365759776 | bytes 20067356 | solution.py:171
  470.9 8.8 all-gather.13
  487.6 8.6 all-gather.15
  512.8 11.0 fusion.55
  523.8 11.9 convert_reduce_fusion
  568.3 18.3 %all-to-all-done.8 = bf16[4,2,56064]{2,1,0:T(2,128)(2,1)} async-done(((bf16[4,2,56064]{2,1,0:T(2,128)(2,1)}), bf16[4,2,56064]{2,1,0:T(2,128)(2,1)}, u32[]{:S(2)}, u32[]{:S(2)}) %all-to-all-start.8) | async-done | bytes 897056 | tf_op jit(solution)/shard_map/all_to_all | solution.py:290
  603.3 37.7 %while.38 = (s32[]{:T(128)}, bf16[3,584,256]{1,2,0:T(8,128)(2,1)}, bf16[3,584,256]{1,2,0:T(8,128)(2,1)}, bf16[3,584,256]{1,2,0:T(8,128)(2,1)}, bf16[3,584,256]{1...) while((s32[]{:T(128)}, bf16[3,584,256]{1,2,0:T(8,128)(2,1)}, ...), condition=%wide.region_18.19_spmd, body=%wide.region_16.18_spmd.sunk | while | flops 894312448 | bytes 48256832 | solution.py:291
  650.0 26.5 %all-to-all-done.9 = bf16[3,584,256]{2,0,1:T(4,128)(2,1)S(1)} async-done(((bf16[3,584,256]{2,0,1:T(4,128)(2,1)}), bf16[3,584,256]{2,0,1:T(4,128)(2,1)S(1)}, u32[]{:S(2)}, u32[]{:S(2)}) %all-to-all-start.9) | async-done | bytes 897056 | tf_op jit(solution)/shard_map/all_to_all | solution.py:295
  683.4 25.1 %all-to-all-done.10 = bf16[3,584,256]{2,0,1:T(4,128)(2,1)S(1)} async-done(((bf16[3,584,256]{2,0,1:T(4,128)(2,1)}), bf16[3,584,256]{2,0,1:T(4,128)(2,1)S(1)}, u32[]{:S(2)}, u32[]{:S(2)}) %all-to-all-start.10) | async-done | bytes 897056 | tf_op jit(solution)/shard_map/all_to_all | solution.py:296
  717.5 23.9 %all-to-all-done.11 = bf16[3,584,256]{2,0,1:T(4,128)(2,1)S(1)} async-done(((bf16[3,584,256]{2,0,1:T(4,128)(2,1)}), bf16[3,584,256]{2,0,1:T(4,128)(2,1)S(1)}, u32[]{:S(2)}, u32[]{:S(2)}) %all-to-all-start.11) | async-done | bytes 897056 | tf_op jit(solution)/shard_map/all_to_all | solution.py:297
  753.6 14.6 %fusion.54 = f32[1024,4096]{1,0:T(8,128)} fusion(bf16[438,4096]{1,0:T(8,128)(2,1)} %copy-done.57, f32[438,1024]{1,0:T(8,128)S(1)} %copy-done.7, f32[1024]{0:T(1024)S(1)} %bitcast.363, f32[1024]{0:T(1024)S(1)} %bitcast.348, f32[438]{0:T(512)S(1)} %fusion.49, f32[438]{0:T(512)S(1)} %broadcast_multiply_fusion.1), kind=kOutput, calls=%fused_computation.138 | convolution fusion | flops 3676452864 | bytes 22171056 | tf_op jit(solution)/shard_map/dot_general | solution.py:25
  769.4 12.4 fusion.32
  782.0 60.9 %reduce-scatter.5.cloned.1.call-done = f32[128,3072]{1,0:T(8,128)} async-done(((f32[1024,3072]{1,0:T(8,128)}), f32[128,3072]{1,0:T(8,128)}) %reduce-scatter.5.cloned.1.call-update) | async-done | bytes 1572880 | tf_op jit(solution)/shard_map/reduce_scatter | solution.py:314
  842.9 119.8 %reduce-scatter.9.cloned.1.call-done = f32[128,4096]{1,0:T(8,128)} async-done(((f32[1024,4096]{1,0:T(8,128)}), f32[128,4096]{1,0:T(8,128)}) %reduce-scatter.9.cloned.1.call-update) | async-done | bytes 2097168 | tf_op jit(solution)/shard_map/reduce_scatter | solution.py:321
  962.7 119.6 %reduce-scatter.11.cloned.1.call-done = f32[512,1024]{1,0:T(8,128)} async-done(((f32[4096,1024]{1,0:T(8,128)}), f32[512,1024]{1,0:T(8,128)}) %reduce-scatter.11.cloned.1.call-update) | async-done | bytes 2097168 | tf_op jit(solution)/shard_map/reduce_scatter | solution.py:323
  1098.9 25.2 %all-reduce.9 = (f32[1024]{0:T(1024)S(1)}, f32[1024]{0:T(1024)S(1)}, f32[1024]{0:T(1024)S(1)}, f32[1024]{0:T(1024)S(1)}, f32[1024]{0:T(1024)S(1)}, /*index=5*/f3...) all-reduce(f32[1024]{0:T(1024)S(1)} %get-tuple-element.242, ...), channel_id=2, replica_groups=mesh['fsdp'=8,'seq'=4] {'fsdp'}, use_global_device_ids=true, to_apply=%region_22.23.clone | all-reduce | flops 12288 | bytes 98304
  1124.8 15.5 %all-reduce.10 = (f32[128]{0:T(128)}, f32[128]{0:T(128)}, f32[128]{0:T(128)}, f32[128]{0:T(128)}, f32[128]{0:T(128)}, /*index=5*/f32[128]{0:T(128)}, f32[128]{0:T(128)}, f32[512]{0:T(512)}, f32[128]{0:T(128)}) all-reduce(f32[128]{0:T(128)S(1)} %dynamic-slice.1, f32[128]{0:T(128)S(1)} %dynamic-slice.3, ...), channel_id=1, replica_groups=mesh['fsdp'=8,'seq'=4] {'seq'}, use_global_device_ids=true, to_apply=%region_23.24 | all-reduce | flops 1536 | bytes 12288 | tf_op jit(solution)/shard_map/psum | solution.py:341
  1140.3 168.0 %all-reduce.14.cloned.1.call-done = (f32[128,3072]{1,0:T(8,128)}, f32[128,1024]{1,0:T(8,128)}, f32[128,4096]{1,0:T(8,128)}, f32[512,1024]{1,0:T(8,128)}) async-done(((f32[128,3072]{1,0:T(8,128)}, f32[128,1024]{1,0:T(8,128)}, f32[128,4096]{1,0:T(8,128)}, f32[512,1024]{1,0:T(8,128)}), (f32[128,3072]{1,0:T(8,128)}, f32[128,1024]{1,0:T(8,128)}, f32[128,4096]{1,0:T(8,128)}, ...) | async-done | bytes 6291472 | tf_op jit(solution)/shard_map/psum | solution.py:341
  (420 shorter events, 476.4 us)
Async XLA Ops:
  7.2 50.9 %all-gather.26.cloned.1.call-start = ((), (), s32[]{:S(2)}) async-start(), calls=%async_computation.16 | async-start | bytes 7077888 | tf_op jit(solution)/shard_map/all_gather | solution.py:55
  7.9 244.7 %all-gather.28.cloned.1.call-start = ((), (), s32[]{:S(2)}) async-start(), calls=%async_computation.17 | async-start | bytes 2359296 | tf_op jit(solution)/shard_map/all_gather | solution.py:58
  8.7 248.6 %all-gather.32.cloned.1.call-start = ((), (), s32[]{:S(2)}) async-start(), calls=%async_computation.19 | async-start | bytes 9437184 | tf_op jit(solution)/shard_map/all_gather | solution.py:64
  9.4 247.9 %all-gather.30.cloned.1.call-start = ((), (), s32[]{:S(2)}) async-start(), calls=%async_computation.18 | async-start | bytes 9437184 | tf_op jit(solution)/shard_map/all_gather | solution.py:62
  10.2 53.3 %copy-start.8 = (f32[438,1024]{1,0:T(8,128)}, f32[438,1024]{1,0:T(8,128)S(1)}, u32[]{:S(2)}) copy-start(f32[438,1024]{1,0:T(8,128)S(1)} %reshape.348) | copy-start | bytes 5382148
  29.9 290.0 %copy-start.36 = (f32[438]{0:T(512)}, f32[438]{0:T(512)S(1)}, u32[]{:S(2)}) copy-start(f32[438]{0:T(512)S(1)} %div.74) | copy-start | bytes 5260
  30.4 33.1 %copy-start.30 = (f32[438]{0:T(512)}, f32[438]{0:T(512)S(1)}, u32[]{:S(2)}) copy-start(f32[438]{0:T(512)S(1)} %add.237) | copy-start | bytes 5260
  30.4 289.5 %copy-start.38 = (f32[438]{0:T(512)}, f32[438]{0:T(512)S(1)}, u32[]{:S(2)}) copy-start(f32[438]{0:T(512)S(1)} %rsqrt.31) | copy-start | bytes 5260
  74.4 27.7 %all-to-all-start = ((bf16[4,2,56064]{2,1,0:T(2,128)(2,1)}), bf16[4,2,56064]{2,1,0:T(2,128)(2,1)}, u32[]{:S(2)}, u32[]{:S(2)}) async-start(bf16[4,2,56064]{2,1,0:T(2,128)(2,1)} %reshape.416), calls=%async_computation | async-start | bytes 1794048 | tf_op jit(solution)/shard_map/all_to_all | solution.py:169
  102.1 26.3 %all-to-all-start.1 = ((bf16[4,2,56064]{2,1,0:T(2,128)(2,1)}), bf16[4,2,56064]{2,1,0:T(2,128)(2,1)}, u32[]{:S(2)}, u32[]{:S(2)}) async-start(bf16[4,2,56064]{2,1,0:T(2,128)(2,1)} %reshape.418), calls=%async_computation.1 | async-start | bytes 1794048 | tf_op jit(solution)/shard_map/all_to_all | solution.py:167
  128.5 26.5 %all-to-all-start.2 = ((bf16[4,2,56064]{2,1,0:T(2,128)(2,1)}), bf16[4,2,56064]{2,1,0:T(2,128)(2,1)}, u32[]{:S(2)}, u32[]{:S(2)}) async-start(bf16[4,2,56064]{2,1,0:T(2,128)(2,1)} %reshape.420), calls=%async_computation.2 | async-start | bytes 1794048 | tf_op jit(solution)/shard_map/all_to_all | solution.py:168
  200.7 41.3 %copy-start.50 = (bf16[128]{0:T(256)(128)(2,1)S(1)}, bf16[128]{0:T(256)(128)(2,1)}, u32[]{:S(2)}) copy-start(bf16[128]{0:T(256)(128)(2,1)} %param.31) | copy-start | bytes 772
  202.8 47.8 %all-to-all-start.3 = ((bf16[3,584,256]{2,0,1:T(4,128)(2,1)}), bf16[3,584,256]{2,0,1:T(4,128)(2,1)S(1)}, u32[]{:S(2)}, u32[]{:S(2)}) async-start(bf16[3,584,256]{2,0,1:T(4,128)(2,1)} %copy.117), calls=%async_computation.3 | async-start | bytes 2392064 | tf_op jit(solution)/shard_map/all_to_all | solution.py:172
  208.0 111.9 %all-gather.36.cloned.1.call-start = ((), (), s32[]{:S(2)}) async-start(), calls=%async_computation.21 | async-start | bytes 7077888 | tf_op jit(solution)/shard_map/all_gather | solution.py:55
  273.8 233.8 %all-gather.38.cloned.1.call-start = ((), (), s32[]{:S(2)}) async-start(), calls=%async_computation.22 | async-start | bytes 2359296 | tf_op jit(solution)/shard_map/all_gather | solution.py:58
  274.4 238.4 %all-gather.40.cloned.1.call-start = ((), (), s32[]{:S(2)}) async-start(), calls=%async_computation.23 | async-start | bytes 9437184 | tf_op jit(solution)/shard_map/all_gather | solution.py:62
  283.6 41.8 %copy-start.33 = (f32[8,1,128]{2,1,0:T(1,128)}, f32[8,1,128]{2,1,0:T(1,128)S(1)}, u32[]{:S(2)}) copy-start(f32[8,1,128]{2,1,0:T(1,128)S(1)} %convert_element_type.275) | copy-start | bytes 12292
  292.0 33.3 %copy-start.43 = (f32[8,1,128]{2,1,0:T(1,128)}, f32[8,1,128]{2,1,0:T(1,128)S(1)}, u32[]{:S(2)}) copy-start(f32[8,1,128]{2,1,0:T(1,128)S(1)} %convert_element_type.276) | copy-start | bytes 12292
  336.2 34.1 %all-to-all-start.6 = ((bf16[4,2,56064]{2,1,0:T(2,128)(2,1)}), bf16[4,2,56064]{2,1,0:T(2,128)(2,1)}, u32[]{:S(2)}, u32[]{:S(2)}) async-start(bf16[4,2,56064]{2,1,0:T(2,128)(2,1)} %reshape.422), calls=%async_computation.6 | async-start | bytes 1794048 | tf_op jit(solution)/shard_map/all_to_all | solution.py:168
  340.7 183.1 %all-gather.34.cloned.1.call-start = ((), (), s32[]{:S(2)}) async-start(), calls=%async_computation.20 | async-start | bytes 9437184 | tf_op jit(solution)/shard_map/all_gather | solution.py:64
  370.3 28.2 %all-to-all-start.5 = ((bf16[4,2,56064]{2,1,0:T(2,128)(2,1)}), bf16[4,2,56064]{2,1,0:T(2,128)(2,1)}, u32[]{:S(2)}, u32[]{:S(2)}) async-start(bf16[4,2,56064]{2,1,0:T(2,128)(2,1)} %reshape.424), calls=%async_computation.5 | async-start | bytes 1794048 | tf_op jit(solution)/shard_map/all_to_all | solution.py:167
  398.5 27.2 %all-to-all-start.4 = ((bf16[4,2,56064]{2,1,0:T(2,128)(2,1)}), bf16[4,2,56064]{2,1,0:T(2,128)(2,1)}, u32[]{:S(2)}, u32[]{:S(2)}) async-start(bf16[4,2,56064]{2,1,0:T(2,128)(2,1)} %reshape.426), calls=%async_computation.4 | async-start | bytes 1794048 | tf_op jit(solution)/shard_map/all_to_all | solution.py:169
  463.7 40.7 %all-to-all-start.7 = ((bf16[3,584,256]{2,0,1:T(4,128)(2,1)}), bf16[3,584,256]{2,0,1:T(4,128)(2,1)}, u32[]{:S(2)}, u32[]{:S(2)}) async-start(bf16[3,584,256]{2,0,1:T(4,128)(2,1)} %copy.132), calls=%async_computation.7 | async-start | bytes 2392064 | tf_op jit(solution)/shard_map/all_to_all | solution.py:172
  558.3 28.2 %all-to-all-start.8 = ((bf16[4,2,56064]{2,1,0:T(2,128)(2,1)}), bf16[4,2,56064]{2,1,0:T(2,128)(2,1)}, u32[]{:S(2)}, u32[]{:S(2)}) async-start(bf16[4,2,56064]{2,1,0:T(2,128)(2,1)} %reshape.428), calls=%async_computation.8 | async-start | bytes 1794048 | tf_op jit(solution)/shard_map/all_to_all | solution.py:290
  563.4 218.6 %reduce-scatter.7.cloned.1.call-start = ((), (), s32[]{:S(2)}) async-start(), calls=%async_computation.25 | async-start | bytes 4718592 | tf_op jit(solution)/shard_map/reduce_scatter | solution.py:317
  644.4 32.2 %all-to-all-start.9 = ((bf16[3,584,256]{2,0,1:T(4,128)(2,1)}), bf16[3,584,256]{2,0,1:T(4,128)(2,1)S(1)}, u32[]{:S(2)}, u32[]{:S(2)}) async-start(bf16[3,584,256]{2,0,1:T(4,128)(2,1)} %copy.142), calls=%async_computation.9 | async-start | bytes 2392064 | tf_op jit(solution)/shard_map/all_to_all | solution.py:295
  676.5 31.9 %all-to-all-start.10 = ((bf16[3,584,256]{2,0,1:T(4,128)(2,1)}), bf16[3,584,256]{2,0,1:T(4,128)(2,1)S(1)}, u32[]{:S(2)}, u32[]{:S(2)}) async-start(bf16[3,584,256]{2,0,1:T(4,128)(2,1)} %copy.145), calls=%async_computation.10 | async-start | bytes 2392064 | tf_op jit(solution)/shard_map/all_to_all | solution.py:296
  709.5 31.9 %all-to-all-start.11 = ((bf16[3,584,256]{2,0,1:T(4,128)(2,1)}), bf16[3,584,256]{2,0,1:T(4,128)(2,1)S(1)}, u32[]{:S(2)}, u32[]{:S(2)}) async-start(bf16[3,584,256]{2,0,1:T(4,128)(2,1)} %copy.148), calls=%async_computation.11 | async-start | bytes 2392064 | tf_op jit(solution)/shard_map/all_to_all | solution.py:297
  713.0 129.8 %reduce-scatter.5.cloned.1.call-start = ((), (), s32[]{:S(2)}) async-start(), calls=%async_computation.24 | async-start | bytes 14155776 | tf_op jit(solution)/shard_map/reduce_scatter | solution.py:314
  752.1 210.6 %reduce-scatter.9.cloned.1.call-start = ((), (), s32[]{:S(2)}) async-start(), calls=%async_computation.26 | async-start | bytes 18874368 | tf_op jit(solution)/shard_map/reduce_scatter | solution.py:321
  768.2 314.2 %reduce-scatter.11.cloned.1.call-start = ((), (), s32[]{:S(2)}) async-start(), calls=%async_computation.27 | async-start | bytes 18874368 | tf_op jit(solution)/shard_map/reduce_scatter | solution.py:323
  781.8 526.6 %all-reduce.14.cloned.1.call-start = ((), (), s32[]{:S(2)}) async-start(), calls=%async_computation.28 | async-start | bytes 12582912 | tf_op jit(solution)/shard_map/psum | solution.py:341
  (51 other events, 272.2 us)
Sparse Core Ops, SparseCore 0:
  9.9 48.1 all-gather.25
  59.9 27.7 all-gather.27
  89.6 54.2 all-gather.31
  145.7 54.2 all-gather.29
  274.0 45.8 all-gather.35
  321.6 27.7 all-gather.37
  351.3 54.2 all-gather.39
  407.5 54.2 all-gather.33
  568.4 51.6 reduce-scatter.6
  752.2 90.6 reduce-scatter.4
  846.5 116.1 reduce-scatter.8
  966.1 116.1 reduce-scatter.10
  1084.9 223.3 all-reduce.13
where the time goes:
time: 1330 us; the launch traced here: 1320 us
  waiting for transfers between devices  647 us (49%)
  local copies, waits for them, and re-layouts  227 us (17%)
  blocking collectives  186 us (14%)
  matrix products  162 us (12%)
  starting transfers between devices  54.2 us (4%)
  other arithmetic  28.8 us (2%)
  between operations  16.4 us (1%)
    psum x1, waiting for transfers between devices, on_device(): lax.psum((part_g1, part_s1, part_qkv, part_qb, part_vb, part_ow, part_ob,...  168 us
    reduce_scatter x1, waiting for transfers between devices, on_device(): lax.psum_scatter(fc1_weight_grad, 'fsdp', scatter_dimension=0, tiled=True)  120 us
    reduce_scatter x1, waiting for transfers between devices, on_device(): lax.psum_scatter(fc2_weight_grad, 'fsdp', scatter_dimension=0, tiled=True)  120 us
    unnamed x160, local copies, waits for them, and re-layouts  96.2 us
    reduce_scatter x1, waiting for transfers between devices, on_device(): lax.psum_scatter(qkv_weight_grad, 'fsdp', scatter_dimension=0, tiled=True)  60.9 us
    while x14, local copies, waits for them, and re-layouts, forward_pass(): lax.map(attend_one, (query_heads, key_heads, value_heads, counts))  44.9 us
    all_gather x2, waiting for transfers between devices, collect(): lax.all_gather(qkv_weight, 'fsdp', axis=0, tiled=True)  38.6 us
    dot_general x4, matrix products, inner_rows(): lax.dot_general(left, right, (((0,), (0,)), ((), ())), preferred_element_...  38.5 us
  transfers between devices with their start and end apart: 25, of which 14 were waited for; matrix products, arithmetic and copies ran while one was open for 26% of the time, Pallas kernels for 0%

commit v1 on v0

v1 whole, which is shorter than its diff:
```python
import functools

import jax
import jax.numpy as jnp
from jax import lax
from jax.experimental import pallas as pl
from jax.experimental.pallas import tpu as pltpu
from jax.sharding import PartitionSpec as P

HEAD_DIM = 64
EPS = 1e-05
MASKED = -1e30
SCALE = HEAD_DIM ** (-0.5)
F32 = jnp.float32
BF16 = jnp.bfloat16
PIECES = 8
LIMIT = 62 * 1024 * 1024


def call(body, grid, in_specs, out_specs, out_shape, scratch, flops, moved, name):
    return pl.pallas_call(
        body,
        grid_spec=pltpu.PrefetchScalarGridSpec(
            num_scalar_prefetch=1,
            grid=grid,
            in_specs=in_specs,
            out_specs=out_specs,
            scratch_shapes=scratch,
        ),
        out_shape=out_shape,
        compiler_params=pltpu.CompilerParams(
            dimension_semantics=("arbitrary",) * len(grid), vmem_limit_bytes=LIMIT
        ),
        cost_estimate=pl.CostEstimate(flops=flops, bytes_accessed=moved, transcendentals=0),
        name=name,
    )


def whole(shape):
    return pl.BlockSpec(shape, lambda *_: (0,) * len(shape))


def dot_nn(left, right):
    return lax.dot_general(left, right, (((1,), (0,)), ((), ())), preferred_element_type=F32)


def dot_nt(left, right):
    return lax.dot_general(left, right, (((1,), (1,)), ((), ())), preferred_element_type=F32)


def dot_tn(left, right):
    return lax.dot_general(left, right, (((0,), (0,)), ((), ())), preferred_element_type=F32)


def lanes(ref, block, width):
    return ref[:, pl.ds(pl.multiple_of(block * width, 128), width)]


def put_lanes(ref, block, width, value):
    ref[:, pl.ds(pl.multiple_of(block * width, 128), width)] = value


def stats(values):
    average = jnp.mean(values, axis=-1, keepdims=True)
    centered = values - average
    inverse = lax.rsqrt(jnp.mean(centered * centered, axis=-1, keepdims=True) + EPS)
    return centered * inverse, inverse


def stacked(refs, rows=None):
    return jnp.concatenate([r[...] if rows is None else r[:rows, :] for r in refs], axis=0)


def project_body(scal, *refs, paired, rows, unit, n_seq, slot):
    xs = refs[:2] if paired else refs[:1]
    gain, shift, bias = refs[len(xs) : len(xs) + 3]
    weights = refs[len(xs) + 3 : len(xs) + 11]
    out, normed, rel = refs[len(xs) + 11 :]

    @pl.when(pl.program_id(0) == 0)
    def _():
        below = scal[1] + slot < n_seq
        for start in range(0, rows, unit):
            span = pl.ds(start, unit)
            values = xs[0][span, :].astype(F32)
            if paired:
                values = jnp.where(below, values, xs[1][span, :].astype(F32))
            normal, _ = stats(values)
            normed[span, :] = (normal * gain[...] + shift[...]).astype(BF16)
        for r in range(PIECES):
            width = rel.shape[1] // PIECES
            rel[:, r * width : (r + 1) * width] = lanes(normed, scal[0] ^ r, width)

    value = dot_nn(rel[...], stacked(weights, rel.shape[1] // PIECES))
    out[...] = (value + bias[0]).astype(BF16)


def project(scal, xs, gain, shift, bias, pieces, n_seq, slot, unit):
    rows, features = xs[0].shape
    group = features // n_seq
    depth = pieces[0].shape[0]
    return call(
        functools.partial(
            project_body, paired=len(xs) == 2, rows=rows, unit=unit, n_seq=n_seq, slot=slot
        ),
        (3,),
        [whole((rows, features))] * len(xs)
        + [whole((1, features))] * 2
        + [pl.BlockSpec((1, 1, group), lambda j, s: (j, 0, 0))]
        + [pl.BlockSpec((depth, group), lambda j, s: (0, n_seq * j + s[1]))] * PIECES,
        [pl.BlockSpec((rows, group), lambda j, s: (0, j)), whole((rows, features))],
        [
            jax.ShapeDtypeStruct((rows, 3 * group), BF16),
            jax.ShapeDtypeStruct((rows, features), BF16),
        ],
        [pltpu.VMEM((rows, features), BF16)],
        2 * rows * features * 3 * group,
        4 * rows * features + 6 * features * group,
        f"project{slot}",
    )(scal, *xs, gain, shift, bias, *pieces)


def half_masks(unit):
    lane = lax.broadcasted_iota(jnp.int32, (unit, 2 * HEAD_DIM), 1)
    return lane < HEAD_DIM


def split_heads(value, low):
    zero = jnp.zeros_like(value)
    return jnp.concatenate([jnp.where(low, value, zero), jnp.where(low, zero, value)], axis=0)


def join_heads(value, low, unit):
    return jnp.where(low, value[:unit], value[unit:])


def attend_body(scal, *refs, n_seq, unit):
    queries, keys, values = refs[:n_seq], refs[n_seq : 2 * n_seq], refs[2 * n_seq : 3 * n_seq]
    mask, outs, lse = refs[3 * n_seq], refs[3 * n_seq + 1 : 4 * n_seq + 1], refs[-1]
    low = half_masks(unit)
    key = stacked(keys)
    value = stacked(values)
    for s in range(n_seq):
        scores = dot_nt(split_heads(queries[s][...], low), key) * SCALE + mask[0]
        top = jnp.max(scores, axis=-1, keepdims=True)
        weight = jnp.exp(scores - top)
        total = jnp.sum(weight, axis=-1, keepdims=True)
        probs = (weight * (1.0 / total)).astype(BF16)
        outs[s][...] = join_heads(dot_nn(probs, value), low, unit).astype(BF16)
        log_total = top + jnp.log(total)
        lse[0, 0, s * unit : (s + 1) * unit, :] = jnp.where(
            low, log_total[:unit], log_total[unit:]
        )


def qkv_specs(n_seq, unit, pairs):
    specs = []
    for j in range(3):
        specs += [
            pl.BlockSpec((unit, 2 * HEAD_DIM), lambda b, p, s, j=j: (b, pairs * j + p))
        ] * n_seq
    return specs


def attend(scal, projected, mask, unit, images):
    n_seq = len(projected)
    rows, wide = projected[0].shape
    group = wide // 3
    pairs = group // (2 * HEAD_DIM)
    tokens = n_seq * unit
    return call(
        functools.partial(attend_body, n_seq=n_seq, unit=unit),
        (images, pairs),
        qkv_specs(n_seq, unit, pairs) + [pl.BlockSpec((1, 1, tokens), lambda b, p, s: (b, 0, 0))],
        [pl.BlockSpec((unit, 2 * HEAD_DIM), lambda b, p, s: (b, p))] * n_seq
        + [pl.BlockSpec((1, 1, tokens, 2 * HEAD_DIM), lambda b, p, s: (b, p, 0, 0))],
        [jax.ShapeDtypeStruct((rows, group), BF16)] * n_seq
        + [jax.ShapeDtypeStruct((images, pairs, tokens, 2 * HEAD_DIM), F32)],
        [],
        images * pairs * 2 * tokens * tokens * 2 * HEAD_DIM * 4,
        n_seq * rows * wide * 4,
        "attend",
    )(scal, *projected, *projected, *projected, mask)


def attend_back_body(scal, *refs, n_seq, unit, pairs):
    queries, keys, values = refs[:n_seq], refs[n_seq : 2 * n_seq], refs[2 * n_seq : 3 * n_seq]
    grads = refs[3 * n_seq : 4 * n_seq]
    mask, lse = refs[4 * n_seq : 4 * n_seq + 2]
    outs = refs[4 * n_seq + 2 : 5 * n_seq + 2]
    key_acc, value_acc = refs[-2:]
    pair = pl.program_id(1)
    low = half_masks(unit)
    key = stacked(keys)
    value = stacked(values)
    for s in range(n_seq):
        query = split_heads(queries[s][...], low)
        grad = split_heads(grads[s][...], low)
        scores = dot_nt(query, key) * SCALE + mask[0]
        saved = lse[0, 0, s * unit : (s + 1) * unit, :]
        column = jnp.concatenate([saved[:, :1], saved[:, HEAD_DIM : HEAD_DIM + 1]], axis=0)
        probs = jnp.exp(scores - column)
        grad_probs = dot_nt(grad, value)
        value_part = dot_tn(probs.astype(BF16), grad)
        center = jnp.sum(grad_probs * probs, axis=-1, keepdims=True)
        grad_scores = (probs * (grad_probs - center)).astype(BF16)
        query_grad = join_heads(dot_nn(grad_scores, key), low, unit) * SCALE
        key_part = dot_tn(grad_scores, query)
        put_lanes(outs[s], pair, 2 * HEAD_DIM, query_grad.astype(BF16))
        if s == 0:
            key_acc[...] = key_part
            value_acc[...] = value_part
        else:
            key_acc[...] += key_part
            value_acc[...] += value_part
    for s in range(n_seq):
        span = pl.ds(s * unit, unit)
        put_lanes(outs[s], pairs + pair, 2 * HEAD_DIM, (key_acc[span, :] * SCALE).astype(BF16))
        put_lanes(outs[s], 2 * pairs + pair, 2 * HEAD_DIM, value_acc[span, :].astype(BF16))


def attend_back(scal, projected, grads, mask, lse, unit, images):
    n_seq = len(projected)
    rows, wide = projected[0].shape
    group = wide // 3
    pairs = group // (2 * HEAD_DIM)
    tokens = n_seq * unit
    return call(
        functools.partial(attend_back_body, n_seq=n_seq, unit=unit, pairs=pairs),
        (images, pairs),
        qkv_specs(n_seq, unit, pairs)
        + [pl.BlockSpec((unit, 2 * HEAD_DIM), lambda b, p, s: (b, p))] * n_seq
        + [
            pl.BlockSpec((1, 1, tokens), lambda b, p, s: (b, 0, 0)),
            pl.BlockSpec((1, 1, tokens, 2 * HEAD_DIM), lambda b, p, s: (b, p, 0, 0)),
        ],
        [pl.BlockSpec((unit, wide), lambda b, p, s: (b, 0))] * n_seq,
        [jax.ShapeDtypeStruct((rows, wide), BF16)] * n_seq,
        [pltpu.VMEM((tokens, 2 * HEAD_DIM), F32)] * 2,
        images * pairs * 2 * tokens * tokens * 2 * HEAD_DIM * 10,
        n_seq * rows * wide * 4,
        "attend_back",
    )(scal, *projected, *projected, *projected, *grads, mask, lse)


def mix_body(scal, *refs, n_seq):
    contexts = refs[:n_seq]
    x, bias, gain, shift = refs[n_seq : n_seq + 4]
    weights = refs[n_seq + 4 : n_seq + 12]
    context, mixed, normed, rel = refs[n_seq + 12 :]
    group = contexts[0].shape[1]
    for t in range(n_seq):
        put_lanes(context, lax.rem(scal[1] + n_seq - t, n_seq), group, contexts[t][...])
    width = rel.shape[1] // PIECES
    for r in range(PIECES):
        rel[:, r * width : (r + 1) * width] = lanes(context, scal[0] ^ r, width)
    branch = dot_nn(rel[...], stacked(weights)) + bias[...]
    flag = (scal[2 + pl.program_id(0)] > 0).astype(F32)
    value = x[...].astype(F32) + branch * flag
    mixed[...] = value
    normal, _ = stats(value)
    normed[...] = (normal * gain[...] + shift[...]).astype(BF16)


def mix(scal, contexts, x, bias, gain, shift, pieces, unit):
    n_seq = len(contexts)
    rows, features = x.shape
    group = features // n_seq
    row_block = pl.BlockSpec((unit, features), lambda b, s: (b, 0))
    return call(
        functools.partial(mix_body, n_seq=n_seq),
        (rows // unit,),
        [pl.BlockSpec((unit, group), lambda b, s: (b, 0))] * n_seq
        + [row_block]
        + [whole((1, features))] * 3
        + [whole(pieces[0].shape)] * PIECES,
        [row_block] * 3,
        [
            jax.ShapeDtypeStruct((rows, features), BF16),
            jax.ShapeDtypeStruct((rows, features), F32),
            jax.ShapeDtypeStruct((rows, features), BF16),
        ],
        [pltpu.VMEM((unit, features), BF16)],
        2 * rows * features * features,
        12 * rows * features + 2 * features * features,
        "mix",
    )(scal, *contexts, x, bias, gain, shift, *pieces)


def widen_body(scal, *refs):
    x, bias = refs[:2]
    weights = refs[2:10]
    active, slope, rel = refs[10:]

    @pl.when(pl.program_id(0) == 0)
    def _():
        width = rel.shape[1] // PIECES
        for r in range(PIECES):
            rel[:, r * width : (r + 1) * width] = lanes(x, scal[0] ^ r, width)

    hidden = dot_nn(rel[...], stacked(weights)) + bias[...]
    gate = jax.nn.sigmoid(1.702 * hidden)
    product = hidden * gate
    active[...] = product.astype(BF16)
    slope[...] = (gate + 1.702 * product * (1.0 - gate)).astype(BF16)


def widen(scal, x, bias, pieces, tile=512):
    rows, features = x.shape
    depth, hidden = pieces[0].shape
    column = pl.BlockSpec((rows, tile), lambda n, s: (0, n))
    return call(
        widen_body,
        (hidden // tile,),
        [whole((rows, features)), pl.BlockSpec((1, tile), lambda n, s: (0, n))]
        + [pl.BlockSpec((depth, tile), lambda n, s: (0, n))] * PIECES,
        [column] * 2,
        [jax.ShapeDtypeStruct((rows, hidden), BF16)] * 2,
        [pltpu.VMEM((rows, features), BF16)],
        2 * rows * features * hidden,
        2 * features * hidden + 4 * rows * hidden,
        "widen",
    )(scal, x, bias, *pieces)


def narrow_body(scal, *refs, unit, keep):
    x, mixed, bias = refs[:3]
    weights = refs[3:11]
    out = refs[11]
    width = weights[0].shape[0]
    total = mixed[...] + bias[...]
    for r in range(PIECES):
        total += dot_nn(lanes(x, scal[0] ^ r, width), weights[r][...])
    for b in range(out.shape[0]):
        out[b] = total[b * unit : b * unit + keep].astype(BF16)


def narrow(scal, x, mixed, bias, pieces, unit, keep, tile=256):
    rows, hidden = x.shape
    depth, features = pieces[0].shape
    images = rows // unit
    return call(
        functools.partial(narrow_body, unit=unit, keep=keep),
        (features // tile,),
        [
            whole((rows, hidden)),
            pl.BlockSpec((rows, tile), lambda n, s: (0, n)),
            pl.BlockSpec((1, tile), lambda n, s: (0, n)),
        ]
        + [pl.BlockSpec((depth, tile), lambda n, s: (0, n))] * PIECES,
        pl.BlockSpec((images, keep, tile), lambda n, s: (0, 0, n)),
        jax.ShapeDtypeStruct((images, keep, features), BF16),
        [],
        2 * rows * features * hidden,
        2 * features * hidden + 2 * rows * hidden + 6 * rows * features,
        "narrow",
    )(scal, x, mixed, bias, *pieces)


def outer_rows_body(scal, left, right, *refs):
    value = dot_tn(left[...], right[...])
    if len(refs) == 2:
        value += refs[0][0].astype(F32)
    refs[-1][0] = value.astype(BF16)


def outer_rows(scal, left, right, offset, added=None):
    rows, hidden = left.shape
    width = hidden // PIECES
    features = right.shape[1]
    block = pl.BlockSpec((1, width, features), lambda m, s: (m, 0, 0))
    half = PIECES // 2
    return call(
        outer_rows_body,
        (half,),
        [
            pl.BlockSpec((rows, width), lambda m, s: (0, s[0] ^ (2 * m + offset))),
            whole((rows, features)),
        ]
        + ([block] if offset == 0 else []),
        block,
        jax.ShapeDtypeStruct((half, width, features), BF16),
        [],
        rows * hidden * features,
        hidden * features * (1 if offset else 2),
        f"outer_rows{offset}",
    )(scal, left, right, *(() if added is None else (added,)))


def outer_body(scal, *refs, count, offset, width):
    lefts, rights = refs[:count], refs[count : 2 * count]
    out, rel = refs[-2:]
    half = PIECES // 2

    @pl.when(pl.program_id(0) == 0)
    def _():
        rows = lefts[0].shape[0]
        for i in range(count):
            for m in range(half):
                rel[i * rows : (i + 1) * rows, m * width : (m + 1) * width] = lanes(
                    lefts[i], scal[0] ^ (2 * m + offset), width
                )

    right = stacked(rights)
    value = dot_tn(rel[...], right)
    for m in range(half):
        part = value[m * width : (m + 1) * width]
        if offset == 0:
            part = part + refs[2 * count][m].astype(F32)
        out[m] = part.astype(BF16)


def outer(scal, lefts, rights, offset, tile, added=None, name=""):
    count = len(lefts)
    rows, features = lefts[0].shape
    wide = rights[0].shape[1]
    width = features // PIECES
    half = PIECES // 2
    block = pl.BlockSpec((half, width, tile), lambda n, s: (0, 0, n))
    return call(
        functools.partial(outer_body, count=count, offset=offset, width=width),
        (wide // tile,),
        [whole((rows, features))] * count
        + [pl.BlockSpec((rows, tile), lambda n, s: (0, n))] * count
        + ([block] if offset == 0 else []),
        block,
        jax.ShapeDtypeStruct((half, width, wide), BF16),
        [pltpu.VMEM((count * rows, half * width), BF16)],
        count * rows * features * wide,
        features * wide * (1 if offset else 2) + count * 2 * rows * (features + wide),
        f"outer_{name}{offset}",
    )(scal, *lefts, *rights, *(() if added is None else (added,)))


def narrow_back_body(scal, *refs):
    grad, slope = refs[:2]
    weights = refs[2:10]
    out = refs[10]
    step = pl.program_id(0)
    part = weights[0].shape[0]
    per = pl.num_programs(0)
    value = dot_nt(grad[...], stacked(weights))
    for r in range(PIECES):
        block = (scal[0] ^ r) * per + step
        put_lanes(
            out,
            block,
            part,
            (value[:, r * part : (r + 1) * part] * lanes(slope, block, part).astype(F32)).astype(
                BF16
            ),
        )


def narrow_back(scal, grad, slope, pieces, steps=4):
    rows, features = grad.shape
    depth = pieces[0].shape[0]
    hidden = slope.shape[1]
    return call(
        narrow_back_body,
        (steps,),
        [whole((rows, features)), whole((rows, hidden))]
        + [pl.BlockSpec((depth // steps, features), lambda n, s: (n, 0))] * PIECES,
        whole((rows, hidden)),
        jax.ShapeDtypeStruct((rows, hidden), BF16),
        [],
        2 * rows * features * hidden,
        2 * features * hidden + 4 * rows * hidden,
        "narrow_back",
    )(scal, grad, slope, *pieces)


def norm_back(grad, normal, inverse, gain):
    scaled = grad * gain
    return inverse * (
        scaled
        - jnp.mean(scaled, axis=-1, keepdims=True)
        - normal * jnp.mean(scaled * normal, axis=-1, keepdims=True)
    )


def rows_sum(value):
    return jnp.sum(value, axis=0, keepdims=True)


def widen_back_body(scal, *refs, unit):
    grad, mixed, dy, gain = refs[:4]
    weights = refs[4:12]
    dmixed, dbranch, sums, bias_sum, acc, nat = refs[12:]
    step = pl.program_id(0)
    value = grad[...]
    bias_sum[...] = rows_sum(value.astype(F32))
    part = dot_nt(value, stacked(weights))

    @pl.when(step == 0)
    def _():
        acc[...] = part

    @pl.when(step > 0)
    def _():
        acc[...] += part

    @pl.when(step == pl.num_programs(0) - 1)
    def _():
        width = acc.shape[1] // PIECES
        totals = [0.0] * 4
        for b in range(acc.shape[0] // unit):
            span = pl.ds(b * unit, unit)
            for r in range(PIECES):
                put_lanes(
                    nat, scal[0] ^ r, width, acc[span, r * width : (r + 1) * width]
                )
            normal, inverse = stats(mixed[span, :])
            grad_out = dy[span, :].astype(F32)
            back = nat[...]
            total = grad_out + norm_back(back, normal, inverse, gain[...])
            dmixed[span, :] = total
            flag = (scal[2 + b] > 0).astype(F32)
            low = (total * flag).astype(BF16)
            dbranch[span, :] = low
            parts = (back * normal, back, low.astype(F32), grad_out)
            totals = [t + rows_sum(p) for t, p in zip(totals, parts)]
        sums[...] = jnp.concatenate(totals + [jnp.zeros((4, acc.shape[1]), F32)], axis=0)


def widen_back(scal, grad, mixed, dy, gain, pieces, unit, tile=1024):
    rows, hidden = grad.shape
    depth = pieces[0].shape[0]
    features = mixed.shape[1]
    full = whole((rows, features))
    return call(
        functools.partial(widen_back_body, unit=unit),
        (hidden // tile,),
        [pl.BlockSpec((rows, tile), lambda n, s: (0, n)), full, full, whole((1, features))]
        + [pl.BlockSpec((depth, tile), lambda n, s: (0, n))] * PIECES,
        [
            full,
            full,
            whole((8, features)),
            pl.BlockSpec((1, tile), lambda n, s: (0, n)),
        ],
        [
            jax.ShapeDtypeStruct((rows, features), F32),
            jax.ShapeDtypeStruct((rows, features), BF16),
            jax.ShapeDtypeStruct((8, features), F32),
            jax.ShapeDtypeStruct((1, hidden), F32),
        ],
        [pltpu.VMEM((rows, features), F32), pltpu.VMEM((unit, features), F32)],
        2 * rows * features * hidden,
        2 * features * hidden + 2 * rows * hidden + 12 * rows * features,
        "widen_back",
    )(scal, grad, mixed, dy, gain, *pieces)


def mix_back_body(scal, *refs, n_seq):
    grad = refs[0]
    weights = refs[1:9]
    outs, rel = refs[9 : 9 + n_seq], refs[-1]
    rel[...] = dot_nt(grad[...], stacked(weights)).astype(BF16)
    width = rel.shape[1] // PIECES
    per = PIECES // n_seq
    for t in range(n_seq):
        owner = lax.rem(scal[1] + t, n_seq)
        for k in range(per):
            outs[t][:, k * width : (k + 1) * width] = lanes(
                rel, scal[0] ^ (owner * per + k), width
            )


def mix_back(scal, grad, pieces, n_seq):
    rows, features = grad.shape
    group = features // n_seq
    return call(
        functools.partial(mix_back_body, n_seq=n_seq),
        (1,),
        [whole((rows, features))] + [whole(pieces[0].shape)] * PIECES,
        [whole((rows, group))] * n_seq,
        [jax.ShapeDtypeStruct((rows, group), BF16)] * n_seq,
        [pltpu.VMEM((rows, features), BF16)],
        2 * rows * features * features,
        4 * rows * features + 2 * features * features,
        "mix_back",
    )(scal, grad, *pieces)


def project_back_body(scal, *refs, n_seq, unit, keep):
    grads = refs[:n_seq]
    x, dmixed, gain = refs[n_seq : n_seq + 3]
    weights = refs[n_seq + 3 : n_seq + 11]
    out, sums, acc, nat, wide = refs[n_seq + 11 :]
    step = pl.program_id(0)
    width = acc.shape[1] // PIECES
    for t in range(n_seq):
        put_lanes(
            wide, lax.rem(scal[1] + n_seq - t, n_seq), grads[t].shape[1], grads[t][...]
        )
    part = dot_nt(wide[...], stacked(weights, width))

    @pl.when(step == 0)
    def _():
        acc[...] = part

    @pl.when(step > 0)
    def _():
        acc[...] += part

    @pl.when(step == pl.num_programs(0) - 1)
    def _():
        totals = [0.0] * 2
        for b in range(acc.shape[0] // unit):
            span = pl.ds(b * unit, unit)
            for r in range(PIECES):
                put_lanes(
                    nat, scal[0] ^ r, width, acc[span, r * width : (r + 1) * width]
                )
            normal, inverse = stats(x[span, :].astype(F32))
            back = nat[...]
            total = dmixed[span, :] + norm_back(back, normal, inverse, gain[...])
            out[b] = total[:keep]
            totals = [t + rows_sum(p) for t, p in zip(totals, (back * normal, back))]
        sums[...] = jnp.concatenate(totals + [jnp.zeros((6, acc.shape[1]), F32)], axis=0)


def project_back(scal, grads, x, dmixed, gain, pieces, unit, keep):
    n_seq = len(grads)
    rows, features = x.shape
    group = features // n_seq
    depth = pieces[0].shape[0]
    images = rows // unit
    full = whole((rows, features))
    return call(
        functools.partial(project_back_body, n_seq=n_seq, unit=unit, keep=keep),
        (3,),
        [pl.BlockSpec((rows, group), lambda j, s: (0, j))] * n_seq
        + [full, full, whole((1, features))]
        + [pl.BlockSpec((depth, features), lambda j, s: (0, j))] * PIECES,
        [whole((images, keep, features)), whole((8, features))],
        [
            jax.ShapeDtypeStruct((images, keep, features), F32),
            jax.ShapeDtypeStruct((8, features), F32),
        ],
        [
            pltpu.VMEM((rows, features), F32),
            pltpu.VMEM((unit, features), F32),
            pltpu.VMEM((rows, features), BF16),
        ],
        6 * rows * features * features,
        6 * features * features + 16 * rows * features,
        "project_back",
    )(scal, *grads, x, dmixed, gain, *pieces)


def flip(value, bit):
    return lax.ppermute(value, "fsdp", [(i, i ^ bit) for i in range(PIECES)])


def flip_mixed(value):
    return lax.ppermute(
        value, "fsdp", [(i, i ^ (4 if i & 1 else 2)) for i in range(PIECES)]
    )


def gather_pieces(shard, odd):
    along_x = flip(shard, 2)
    along_y = flip(shard, 4)
    far = flip_mixed(jnp.where(odd, along_x, along_y))
    pieces = []
    for piece in (shard, along_x, along_y, far):
        pieces += [piece, flip(piece, 1)]
    return pieces


def gather_whole(shard):
    full = lax.all_gather(shard, "fsdp", axis=0, tiled=True)
    size = full.shape[0] // PIECES
    return [full[r * size : (r + 1) * size] for r in range(PIECES)]


def add32(*values):
    total = values[0].astype(F32)
    for value in values[1:]:
        total = total + value.astype(F32)
    return total


def scatter_pieces(theirs_fn, mine_fn, odd):
    theirs = theirs_fn()
    summed = mine_fn(flip(theirs, 1))
    passed = flip_mixed(summed[3])
    none = jnp.zeros_like(passed)
    to_x = add32(summed[1], jnp.where(odd, passed, none)).astype(BF16)
    to_y = add32(summed[2], jnp.where(odd, none, passed)).astype(BF16)
    return add32(summed[0], flip(to_x, 2), flip(to_y, 4))


def scatter_whole(theirs_fn, mine_fn):
    theirs = theirs_fn()
    mine = mine_fn(jnp.zeros_like(theirs))
    full = jnp.stack([mine, theirs], axis=1)
    full = full.reshape(PIECES * full.shape[2], full.shape[3])
    return lax.psum_scatter(full.astype(F32), "fsdp", scatter_dimension=0, tiled=True)


def swap_seq(value, bit, n_seq):
    return lax.ppermute(value, "seq", [(i, i ^ bit) for i in range(n_seq)])


def shift_seq(value, amount, n_seq):
    return lax.ppermute(value, "seq", [(i, (i + amount) % n_seq) for i in range(n_seq)])


def sum_seq(value, place, n_seq):
    bits = [1 << k for k in range(n_seq.bit_length() - 1)]
    for bit in bits:
        half = value.shape[0] // 2
        upper = (place & bit) != 0
        first, second = value[:half], value[half:]
        sent = jnp.where(upper, first, second).astype(BF16)
        value = jnp.where(upper, second, first).astype(F32) + swap_seq(sent, bit, n_seq)
    value = value.astype(BF16)
    for bit in reversed(bits):
        upper = (place & bit) != 0
        other = swap_seq(value, bit, n_seq)
        value = jnp.concatenate(
            [jnp.where(upper, other, value), jnp.where(upper, value, other)], axis=0
        )
    return value.astype(F32)


def butterfly(value, n_fsdp, n_seq):
    for bit in (1 << k for k in range(n_fsdp.bit_length() - 1)):
        value = value + lax.ppermute(value, "fsdp", [(i, i ^ bit) for i in range(n_fsdp)])
    for bit in (1 << k for k in range(n_seq.bit_length() - 1)):
        value = value + swap_seq(value, bit, n_seq)
    return value


def line_gather(x, n_seq):
    ups, downs = [], []
    up = down = x
    for t in range(1, n_seq):
        up = lax.ppermute(up, "seq", [(i, i + 1) for i in range(t - 1, n_seq - 1)])
        down = lax.ppermute(down, "seq", [(i + 1, i) for i in range(0, n_seq - t)])
        ups.append(up)
        downs.append(down)
    return [(x,)] + [(downs[t - 1], ups[n_seq - t - 1]) for t in range(1, n_seq)]


def on_device(
    n_fsdp,
    n_seq,
    tokens,
    counts,
    norm1_gain,
    norm1_shift,
    qkv_weight,
    query_bias,
    value_bias,
    out_weight,
    out_bias,
    norm2_gain,
    norm2_shift,
    fc1_weight,
    fc1_bias,
    fc2_weight,
    fc2_bias,
    cotangent,
):
    images, local_len, features = tokens.shape
    hidden = fc1_weight.shape[1]
    unit = -(-local_len // 16) * 16
    group = features // n_seq
    shard = lax.axis_index("fsdp")
    place = lax.axis_index("seq")
    cross = n_fsdp == PIECES
    odd = (shard & 1) == 1
    me = shard if cross else jnp.zeros_like(shard)
    scal = jnp.concatenate([jnp.stack([me, place]).astype(jnp.int32), counts])
    gather = functools.partial(gather_pieces, odd=odd) if cross else gather_whole
    scatter = functools.partial(scatter_pieces, odd=odd) if cross else scatter_whole

    padding = ((0, 0), (0, unit - local_len), (0, 0))
    x = jnp.pad(tokens, padding).reshape(images * unit, features)
    dy = jnp.pad(cotangent, padding).reshape(images * unit, features)

    vectors = (
        norm1_gain,
        norm1_shift,
        query_bias,
        value_bias,
        out_bias,
        norm2_gain,
        norm2_shift,
        fc2_bias,
        fc1_bias,
    )
    if cross:
        packed = jnp.concatenate(vectors)
        extra = jnp.pad(packed[None], ((0, 15), (0, qkv_weight.shape[1] - packed.shape[0])))
        qkv_pieces = gather(jnp.concatenate([qkv_weight, extra], axis=0))
        depth = features // PIECES
        held = jnp.stack([p[depth, : packed.shape[0]] for p in qkv_pieces]).astype(F32)
        order = jnp.arange(PIECES)
        match = (order[:, None] ^ me) == order[None, :]
        held = jnp.sum(jnp.where(match[:, :, None], held[None], 0.0), axis=1)
        full, at = [], 0
        for v in vectors:
            full.append(held[:, at : at + v.shape[0]].reshape(1, -1))
            at += v.shape[0]
    else:
        qkv_pieces = gather(qkv_weight)
        full = [
            lax.all_gather(v, "fsdp", axis=0, tiled=True).astype(F32).reshape(1, -1)
            for v in vectors
        ]
    gain1, shift1, bias_q, bias_v, bias_o, gain2, shift2, bias_2, bias_1 = full
    slots = line_gather(x, n_seq)
    out_pieces = gather(out_weight)
    fc1_pieces = gather(fc1_weight)
    fc2_pieces = gather(fc2_weight)

    own = lambda v: lax.dynamic_slice_in_dim(v, place * group, group, axis=1)
    bias = jnp.stack([own(bias_q), jnp.zeros((1, group), F32), own(bias_v)])

    spot = jnp.arange(n_seq * unit)
    owner = (spot // unit + place) % n_seq
    inside = spot % unit
    position = owner * local_len + inside
    mask = jnp.where(position[None] < counts[:, None], 0.0, MASKED)
    mask = jnp.where(inside[None] < local_len, mask, 2 * MASKED).astype(F32)[:, None]

    projected, normed = [], []
    for s in range(n_seq):
        out, h = project(scal, slots[s], gain1, shift1, bias, qkv_pieces, n_seq, s, unit)
        projected.append(out)
        normed.append(h)
    *contexts, lse = attend(scal, projected, mask, unit, images)
    contexts = [contexts[0]] + [shift_seq(contexts[t], t, n_seq) for t in range(1, n_seq)]
    context, mixed, normed_two = mix(
        scal, contexts, x, bias_o, gain2, shift2, out_pieces, unit
    )
    active, slope = widen(scal, normed_two, bias_1, fc1_pieces)
    output = narrow(scal, active, mixed, bias_2, fc2_pieces, unit, local_len)

    fc2_sum = scatter(
        lambda: outer_rows(scal, active, dy, 1), lambda a: outer_rows(scal, active, dy, 0, a)
    )
    grad_hidden = narrow_back(scal, dy, slope, fc2_pieces)
    fc1_sum = scatter(
        lambda: outer(scal, [normed_two], [grad_hidden], 1, 512, None, "wide"),
        lambda a: outer(scal, [normed_two], [grad_hidden], 0, 512, a, "wide"),
    )
    dmixed, dbranch, sums2, fc1_bias_sum = widen_back(
        scal, grad_hidden, mixed, dy, gain2, fc1_pieces, unit
    )
    grads = mix_back(scal, dbranch, out_pieces, n_seq)
    arrived = [grads[0]] + [
        shift_seq(grads[t], t, n_seq) for t in range(1, n_seq)
    ]
    arrived = [arrived[(n_seq - s) % n_seq] for s in range(n_seq)]
    out_sum = scatter(
        lambda: outer(scal, [context], [dbranch], 1, 512, None, "mix"),
        lambda a: outer(scal, [context], [dbranch], 0, 512, a, "mix"),
    )
    back = attend_back(scal, projected, arrived, mask, lse, unit, images)
    returned = [back[0]] + [shift_seq(back[t], t, n_seq) for t in range(1, n_seq)]
    qkv_sum = scatter(
        lambda: outer(scal, normed, back, 1, group, None, "qkv"),
        lambda a: outer(scal, normed, back, 0, group, a, "qkv"),
    )
    input_grad, sums1 = project_back(
        scal, returned, x, dmixed, gain1, qkv_pieces, unit, local_len
    )

    fc2_weight_grad = sum_seq(fc2_sum, place, n_seq)
    fc1_weight_grad = sum_seq(fc1_sum, place, n_seq)
    out_weight_grad = sum_seq(out_sum, place, n_seq)
    low = qkv_sum.astype(BF16)
    parts = [low] + [shift_seq(low, t, n_seq) for t in range(1, n_seq)]
    parts = [p.reshape(-1, 3, 1, group) for p in parts]
    where_from = (place - jnp.arange(n_seq)) % n_seq
    qkv_weight_grad = sum(
        jnp.where(
            (where_from[t] == jnp.arange(n_seq))[None, None, :, None], parts[t].astype(F32), 0.0
        )
        for t in range(n_seq)
    ).reshape(-1, 3 * features)

    heads_sum = sum(jnp.sum(b.astype(F32), axis=0) for b in back).reshape(3, group)
    spread = lambda v: lax.dynamic_update_slice_in_dim(
        jnp.zeros((features,), F32), v, place * group, axis=0
    )
    small = jnp.concatenate(
        [
            sums1[0],
            sums1[1],
            spread(heads_sum[0]),
            spread(heads_sum[2]),
            sums2[2],
            sums2[0],
            sums2[1],
            sums2[3],
            fc1_bias_sum[0],
        ]
    )
    small = butterfly(small.reshape(-1, 128), n_fsdp, n_seq).reshape(-1)
    shares, at = [], 0
    for v in vectors:
        size = v.shape[0]
        span = size * n_fsdp
        shares.append(lax.dynamic_slice_in_dim(small[at : at + span], shard * size, size))
        at += span
    g1, s1, qb, vb, ob, g2, s2, b2, b1 = shares
    return (
        output,
        input_grad,
        g1,
        s1,
        qkv_weight_grad,
        qb,
        vb,
        out_weight_grad,
        ob,
        g2,
        s2,
        fc1_weight_grad,
        b1,
        fc2_weight_grad,
        b2,
    )


def solution(mesh):
    rows, vector, matrix = P("fsdp", "seq", None), P("fsdp"), P("fsdp", None)
    return jax.shard_map(
        functools.partial(on_device, mesh.shape["fsdp"], mesh.shape["seq"]),
        mesh=mesh,
        in_specs=(
            rows,
            vector,
            vector,
            vector,
            matrix,
            vector,
            vector,
            matrix,
            vector,
            vector,
            vector,
            matrix,
            vector,
            matrix,
            vector,
            rows,
        ),
        out_specs=(
            rows,
            rows,
            vector,
            vector,
            matrix,
            vector,
            vector,
            matrix,
            vector,
            vector,
            vector,
            matrix,
            vector,
            matrix,
            vector,
        ),
        check_vma=False,
    )
```

time: 1330 us -> 648 us (0.49)
  waiting for transfers between devices: 647 us -> 261 us
  Pallas kernels: 0 us -> 196 us
  blocking collectives: 186 us -> 0 us
  local copies, waits for them, and re-layouts: 227 us -> 56.2 us
  matrix products: 162 us -> 0 us
  starting transfers between devices: 54.2 us -> 96.6 us
  between operations: 16.4 us -> 2.03 us
    reduce_scatter x4 -> x0, waiting for transfers between devices: 300 us -> none  [the longest x1 120 us: on_device(): lax.psum_scatter(fc1_weight_grad, 'fsdp', scatter_dimension=0, tiled=True)]
    ppermute x0 -> x79, waiting for transfers between devices: none -> 261 us  [the longest x36 99.5 us: flip(): return lax.ppermute(value, 'fsdp', [(i, i ^ bit) for i in range(PIECES)])]
    pallas_call x0 -> x21, Pallas kernels: none -> 196 us  [the longest x6 42.8 us: outer(): call(functools.partial(outer_body, count=count, offset=offset, width=widt...]
    psum x1 -> x0, waiting for transfers between devices: 168 us -> none  [on_device(): lax.psum((part_g1, part_s1, part_qkv, part_qb, part_vb, part_ow, part_ob,...]
    dot_general x38 -> x0, matrix products: 148 us -> none  [the longest x4 38.5 us: inner_rows(): lax.dot_general(left, right, (((0,), (0,)), ((), ())), preferred_element_...]
    all_gather x17 -> x0, blocking collectives: 146 us -> none  [the longest x2 18.7 us: collect(): lax.all_gather(norm1_shift, 'fsdp', axis=0, tiled=True)]
    all_to_all x12 -> x0, waiting for transfers between devices: 136 us -> none  [the longest x2 27 us: forward_pass(): lax.all_to_all(query_rows, 'seq', split_axis=2, concat_axis=1, tiled=True)]
    ppermute x0 -> x79, starting transfers between devices: none -> 96.6 us  [the longest x14 29 us: swap_seq(): return lax.ppermute(value, 'seq', [(i, i ^ bit) for i in range(n_seq)])]
  transfers between devices with their start and end apart: 25 -> 79, of which waited for: 14 -> 24; matrix products, arithmetic and copies ran while one was open for 26% -> 11% of each run, Pallas kernels for 0% -> 24%
where the time goes in v1:
time: 648 us; the launch traced here: 641 us
  waiting for transfers between devices  261 us (40%)
  Pallas kernels  196 us (30%)
  starting transfers between devices  96.6 us (15%)
  local copies, waits for them, and re-layouts  56.2 us (9%)
  other arithmetic  30.2 us (5%)
    ppermute x36, waiting for transfers between devices, flip(): return lax.ppermute(value, 'fsdp', [(i, i ^ bit) for i in range(PIECES)])  99.5 us
    ppermute x12, waiting for transfers between devices, shift_seq(): lax.ppermute(value, 'seq', [(i, (i + amount) % n_seq) for i in range(n_se...  63.8 us
    ppermute x14, waiting for transfers between devices, swap_seq(): return lax.ppermute(value, 'seq', [(i, i ^ bit) for i in range(n_seq)])  62.7 us
    pallas_call x6, Pallas kernels, outer(): call(functools.partial(outer_body, count=count, offset=offset, width=widt...  42.8 us
    ppermute x14, starting transfers between devices, swap_seq(): return lax.ppermute(value, 'seq', [(i, i ^ bit) for i in range(n_seq)])  29 us
    pallas_call x4, Pallas kernels, project(): call(functools.partial(project_body, paired=len(xs) == 2, rows=rows, unit...  25.8 us
    ppermute x36, starting transfers between devices, flip(): return lax.ppermute(value, 'fsdp', [(i, i ^ bit) for i in range(PIECES)])  24.3 us
    ppermute x3, waiting for transfers between devices, line_gather(): down = lax.ppermute(down, 'seq', [(i + 1, i) for i in range(0, n_seq - t)])  23 us
  transfers between devices with their start and end apart: 79, of which 24 were waited for; matrix products, arithmetic and copies ran while one was open for 11% of the time, Pallas kernels for 24%

profile of v1, /device:TPU:0, one launch (start us, length us, event | category | flops | bytes accessed | tf_op | source)
XLA Modules:
  0.0 641.2 jit_solution(16209264254954712223)
XLA Ops:
  14.3 23.3 %collective-permute-done.19.refs_12_.refs_5_ = bf16[128,1024]{1,0:T(8,128)(2,1)S(1)} collective-permute-done((bf16[128,1024]{1,0:T(8,128)(2,1)}, bf16[128,1024]{1,0:T(8,128)(2,1)S(1)}, u32[]{:S(2)}, u32[]{:S(2)}) %collective-permute-start.19) | collective-permute-done | bytes 262176 | tf_op jit(solution)/shard_map/ppermute | solution.py:654
  49.6 13.5 %collective-permute-done.1.refs_6_.refs_7_.refs_9_ = bf16[144,3072]{1,0:T(8,128)(2,1)S(1)} collective-permute-done((bf16[144,3072]{1,0:T(8,128)(2,1)S(1)}, bf16[144,3072]{1,0:T(8,128)(2,1)S(1)}, u32[]{:S(2)}, u32[]{:S(2)}) %collective-permute-start.1) | collective-permute-done | bytes 884768 | tf_op jit(solution)/shard_map/ppermute | solution.py:654
  76.5 13.0 %collective-permute-done.24.refs_4_.refs_6_ = bf16[128,4096]{1,0:T(8,128)(2,1)} collective-permute-done((bf16[128,4096]{1,0:T(8,128)(2,1)}, bf16[128,4096]{1,0:T(8,128)(2,1)}, u32[]{:S(2)}, u32[]{:S(2)}) %collective-permute-start.24) | collective-permute-done | bytes 1048608 | tf_op jit(solution)/shard_map/ppermute | solution.py:654
  93.4 15.9 %collective-permute-done.31.refs_5_.refs_4_ = bf16[512,1024]{1,0:T(8,128)(2,1)S(1)} collective-permute-done((bf16[512,1024]{1,0:T(8,128)(2,1)}, bf16[512,1024]{1,0:T(8,128)(2,1)S(1)}, u32[]{:S(2)}, u32[]{:S(2)}) %collective-permute-start.31) | collective-permute-done | bytes 1048608 | tf_op jit(solution)/shard_map/ppermute | solution.py:654
  109.2 9.5 %collective-permute-done.5.refs_10_.refs_11_.refs_13_ = bf16[144,3072]{1,0:T(8,128)(2,1)S(1)} collective-permute-done((bf16[144,3072]{1,0:T(8,128)(2,1)S(1)}, bf16[144,3072]{1,0:T(8,128)(2,1)S(1)}, u32[]{:S(2)}, u32[]{:S(2)}) %collective-permute-start.5) | collective-permute-done | bytes 884768 | tf_op jit(solution)/shard_map/ppermute | solution.py:658
  128.2 18.5 %collective-permute-done.12.refs_0_ = bf16[480,1024]{1,0:T(8,128)(2,1)} collective-permute-done((bf16[480,1024]{1,0:T(8,128)(2,1)}, bf16[480,1024]{1,0:T(8,128)(2,1)}, u32[]{:S(2)}, u32[]{:S(2)}) %collective-permute-start.12) | collective-permute-done | bytes 983072 | tf_op jit(solution)/shard_map/ppermute | solution.py:743
  168.0 6.6 %project3.1 = (bf16[480,768]{1,0:T(8,128)(2,1)}, bf16[480,1024]{1,0:T(8,128)(2,1)}) custom-call(s32[5]{0:T(128)} %pad_add_fusion.scal, bf16[480,1024]{1,0:T(8,128)(2,1)} %collective-permute-done.12.refs_0_, bf16[480,1024]{1,0:T(8,128)(2,1)} %collective-permute-done.8.refs_1_, f32[1,1024]{1,0:T(1,128)} %bitcast.138, f32[1,1024]{1,0:T(1,128)} %bitcast.143, ...), custom_call_target="tpu_custom_call" | custom-call | flops 754974720 | bytes 3538944 | tf_op jit(solution)/shard_map/project3/pallas_call | solution.py:102
  174.7 18.1 %attend.1 = (bf16[480,256]{1,0:T(8,128)(2,1)}, bf16[480,256]{1,0:T(8,128)(2,1)}, bf16[480,256]{1,0:T(8,128)(2,1)}, bf16[480,256]{1,0:T(8,128)(2,1)}, f32[3,2,640,128]{3,2,1,0:T(8,128)}) custom-call(s32[5]{0:T(128)} %pad_add_fusion.scal, bf16[480,768]{1,0:T(8,128)(2,1)} %get-tuple-element.47.refs_0_.refs_4_.refs_8_, ...), custom_call_target="tpu_custom_call" | custom-call | flops 2516582400 | bytes 5898240 | tf_op jit(solution)/shard_map/attend/pallas_call | solution.py:171
  204.6 9.2 %collective-permute-done.14.refs_2_ = bf16[480,256]{1,0:T(8,128)(2,1)S(1)} collective-permute-done((bf16[480,256]{1,0:T(8,128)(2,1)}, bf16[480,256]{1,0:T(8,128)(2,1)S(1)}, u32[]{:S(2)}, u32[]{:S(2)}) %collective-permute-start.14) | collective-permute-done | bytes 245792 | tf_op jit(solution)/shard_map/ppermute | solution.py:709
  225.5 13.1 %widen.1 = (bf16[480,4096]{1,0:T(8,128)(2,1)}, bf16[480,4096]{1,0:T(8,128)(2,1)}) custom-call(s32[5]{0:T(128)} %pad_add_fusion.scal, bf16[480,1024]{1,0:T(8,128)(2,1)} %get-tuple-element.55.refs_0_, f32[1,4096]{1,0:T(1,128)} %bitcast.150, bf16[128,4096]{1,0:T(8,128)(2,1)} %refs_4_.1, bf16[128,4096]{1,0:T(8,128)(2,1)} %collective-permute-done.23.refs_3_.refs_5_, ...), custom_call_target="tpu_custom_call" | custom-call | flops 4026531840 | bytes 16252928 | tf_op jit(solution)/shard_map/widen/pallas_call | solution.py:312
  238.7 11.9 %narrow_back.1.refs_0_.refs_1_ = bf16[480,4096]{1,0:T(8,128)(2,1)} custom-call(s32[5]{0:T(128)} %pad_add_fusion.scal, bf16[480,1024]{1,0:T(8,128)(2,1)} %bitcast.126, bf16[480,4096]{1,0:T(8,128)(2,1)} %get-tuple-element.58.refs_1_, bf16[512,1024]{1,0:T(8,128)(2,1)} %refs_2_.3, bf16[512,1024]{1,0:T(8,128)(2,1)} %collective-permute-done.30.refs_4_.refs_3_, ...), custom_call_target="tpu_custom_call" | custom-call | flops 4026531840 | bytes 16252928 | tf_op jit(solution)/shard_map/narrow_back/pallas_call | solution.py:459
  250.5 9.3 %outer_wide1.1 = bf16[4,128,4096]{2,1,0:T(8,128)(2,1)} custom-call(s32[5]{0:T(128)} %pad_add_fusion.scal, bf16[480,1024]{1,0:T(8,128)(2,1)} %get-tuple-element.55.refs_0_, bf16[480,4096]{1,0:T(8,128)(2,1)} %narrow_back.1.refs_0_.refs_1_), custom_call_target="tpu_custom_call" | custom-call | flops 2013265920 | bytes 9109504 | tf_op jit(solution)/shard_map/outer_wide1/pallas_call | solution.py:420
  259.8 13.7 %widen_back.1 = (f32[480,1024]{1,0:T(8,128)}, bf16[480,1024]{1,0:T(8,128)(2,1)}, f32[8,1024]{1,0:T(8,128)}, f32[1,4096]{1,0:T(1,128)}) custom-call(s32[5]{0:T(128)} %pad_add_fusion.scal, bf16[480,4096]{1,0:T(8,128)(2,1)} %narrow_back.1.refs_0_.refs_1_, f32[480,1024]{1,0:T(8,128)} %get-tuple-element.57.refs_1_, bf16[480,1024]{1,0:T(8,128)(2,1)} %bitcast.127, ...), custom_call_target="tpu_custom_call" | custom-call | flops 4026531840 | bytes 18219008 | tf_op jit(solution)/shard_map/widen_back/pallas_call | solution.py:531
  288.0 6.8 %outer_rows1.1 = bf16[4,512,1024]{2,1,0:T(8,128)(2,1)} custom-call(s32[5]{0:T(128)} %pad_add_fusion.scal, bf16[480,4096]{1,0:T(8,128)(2,1)} %get-tuple-element.56.refs_0_.left, bf16[480,1024]{1,0:T(8,128)(2,1)} %bitcast.128), custom_call_target="tpu_custom_call" | custom-call | flops 2013265920 | bytes 4194304 | tf_op jit(solution)/shard_map/outer_rows1/pallas_call | solution.py:373
  295.4 10.8 %collective-permute-done.38.refs_14_ = bf16[480,256]{1,0:T(8,128)(2,1)S(1)} collective-permute-done((bf16[480,256]{1,0:T(8,128)(2,1)}, bf16[480,256]{1,0:T(8,128)(2,1)S(1)}, u32[]{:S(2)}, u32[]{:S(2)}) %collective-permute-start.38) | collective-permute-done | bytes 245792 | tf_op jit(solution)/shard_map/ppermute | solution.py:709
  306.9 22.4 %attend_back.1 = (bf16[480,768]{1,0:T(8,128)(2,1)}, bf16[480,768]{1,0:T(8,128)(2,1)}, bf16[480,768]{1,0:T(8,128)(2,1)}, bf16[480,768]{1,0:T(8,128)(2,1)}) custom-call(s32[5]{0:T(128)} %pad_add_fusion.scal, bf16[480,768]{1,0:T(8,128)(2,1)} %get-tuple-element.47.refs_0_.refs_4_.refs_8_, bf16[480,768]{1,0:T(8,128)(2,1)} %get-tuple-element.48.refs_1_.refs_5_.refs_9_, ...), custom_call_target="tpu_custom_call" | custom-call | flops 6291456000 | bytes 5898240 | tf_op jit(solution)/shard_map/attend_back/pallas_call | solution.py:228
  337.3 7.5 %outer_qkv1.1 = bf16[4,128,768]{2,1,0:T(8,128)(2,1)} custom-call(s32[5]{0:T(128)} %pad_add_fusion.scal, bf16[480,1024]{1,0:T(8,128)(2,1)} %get-tuple-element.74.refs_0_, bf16[480,1024]{1,0:T(8,128)(2,1)} %get-tuple-element.75.refs_1_, bf16[480,1024]{1,0:T(8,128)(2,1)} %get-tuple-element.76.refs_2_, bf16[480,1024]{1,0:T(8,128)(2,1)} %get-tuple-element.77.refs_3_, ...), custom_call_target="tpu_custom_call" | custom-call | flops 1509949440 | bytes 7667712 | tf_op jit(solution)/shard_map/outer_qkv1/pallas_call | solution.py:420
  345.2 7.1 %collective-permute-done.40.refs_1_ = bf16[480,768]{1,0:T(8,128)(2,1)} collective-permute-done((bf16[480,768]{1,0:T(8,128)(2,1)}, bf16[480,768]{1,0:T(8,128)(2,1)}, u32[]{:S(2)}, u32[]{:S(2)}) %collective-permute-start.40) | collective-permute-done | bytes 737312 | tf_op jit(solution)/shard_map/ppermute | solution.py:709
  352.3 30.2 %collective-permute-done.41.refs_2_ = bf16[480,768]{1,0:T(8,128)(2,1)} collective-permute-done((bf16[480,768]{1,0:T(8,128)(2,1)}, bf16[480,768]{1,0:T(8,128)(2,1)}, u32[]{:S(2)}, u32[]{:S(2)}) %collective-permute-start.41) | collective-permute-done | bytes 737312 | tf_op jit(solution)/shard_map/ppermute | solution.py:709
  382.6 11.9 %project_back.1 = (f32[3,146,1024]{2,1,0:T(8,128)}, f32[8,1024]{1,0:T(8,128)}) custom-call(s32[5]{0:T(128)} %pad_add_fusion.scal, bf16[480,768]{1,0:T(8,128)(2,1)} %get-tuple-element.65.refs_0_.refs_4_, bf16[480,768]{1,0:T(8,128)(2,1)} %collective-permute-done.40.refs_1_, bf16[480,768]{1,0:T(8,128)(2,1)} %collective-permute-done.41.refs_2_, ...), custom_call_target="tpu_custom_call" | custom-call | flops 3019898880 | bytes 14155776 | tf_op jit(solution)/shard_map/project_back/pallas_call | solution.py:631
  400.1 7.7 %outer_qkv0.1 = bf16[4,128,768]{2,1,0:T(8,128)(2,1)} custom-call(s32[5]{0:T(128)} %pad_add_fusion.scal, bf16[480,1024]{1,0:T(8,128)(2,1)} %get-tuple-element.74.refs_0_, bf16[480,1024]{1,0:T(8,128)(2,1)} %get-tuple-element.75.refs_1_, bf16[480,1024]{1,0:T(8,128)(2,1)} %get-tuple-element.76.refs_2_, bf16[480,1024]{1,0:T(8,128)(2,1)} %get-tuple-element.77.refs_3_, ...), custom_call_target="tpu_custom_call" | custom-call | flops 1509949440 | bytes 8454144 | tf_op jit(solution)/shard_map/outer_qkv0/pallas_call | solution.py:420
  416.3 15.8 %collective-permute-start.46 = (f32[96,128]{1,0:T(8,128)S(1)}, f32[96,128]{1,0:T(8,128)S(1)}, u32[]{:S(2)}, u32[]{:S(2)}) collective-permute-start(f32[96,128]{1,0:T(8,128)S(1)} %add.189), channel_id=1, source_target_pairs={{0,1},{1,0},{2,3},{3,2},{4,5},{5,4},{6,7},{7,6},{8,9},{9,8},{10,11... | collective-permute-start | bytes 147464 | tf_op jit(solution)/shard_map/ppermute | solution.py:705
  435.8 10.4 %narrow.1 = bf16[3,146,1024]{2,1,0:T(8,128)(2,1)} custom-call(s32[5]{0:T(128)} %pad_add_fusion.scal, bf16[480,4096]{1,0:T(8,128)(2,1)} %get-tuple-element.56.refs_0_.left, f32[480,1024]{1,0:T(8,128)} %get-tuple-element.57.refs_1_, f32[1,1024]{1,0:T(1,128)} %bitcast.146, bf16[512,1024]{1,0:T(8,128)(2,1)} %refs_2_.3, ...), custom_call_target="tpu_custom_call" | custom-call | flops 4026531840 | bytes 15269888 | tf_op jit(solution)/shard_map/narrow/pallas_call | solution.py:342
  465.4 7.5 %outer_rows0.1 = bf16[4,512,1024]{2,1,0:T(8,128)(2,1)} custom-call(s32[5]{0:T(128)} %pad_add_fusion.scal, bf16[480,4096]{1,0:T(8,128)(2,1)} %get-tuple-element.56.refs_0_.left, bf16[480,1024]{1,0:T(8,128)(2,1)} %bitcast.129, bf16[4,512,1024]{2,1,0:T(8,128)(2,1)} %collective-permute-done.71.refs_0_), custom_call_target="tpu_custom_call" | custom-call | flops 2013265920 | bytes 8388608 | tf_op jit(solution)/shard_map/outer_rows0/pallas_call | solution.py:373
  475.8 10.3 %outer_wide0.1 = bf16[4,128,4096]{2,1,0:T(8,128)(2,1)} custom-call(s32[5]{0:T(128)} %pad_add_fusion.scal, bf16[480,1024]{1,0:T(8,128)(2,1)} %get-tuple-element.55.refs_0_, bf16[480,4096]{1,0:T(8,128)(2,1)} %narrow_back.1.refs_0_.refs_1_, bf16[4,128,4096]{2,1,0:T(8,128)(2,1)} %collective-permute-done.63.refs_2_), custom_call_target="tpu_custom_call" | custom-call | flops 2013265920 | bytes 13303808 | tf_op jit(solution)/shard_map/outer_wide0/pallas_call | solution.py:420
  531.5 17.5 %collective-permute-done.73 = bf16[512,1024]{1,0:T(8,128)(2,1)S(1)} collective-permute-done((bf16[512,1024]{1,0:T(8,128)(2,1)S(1)}, bf16[512,1024]{1,0:T(8,128)(2,1)S(1)}, u32[]{:S(2)}, u32[]{:S(2)}) %collective-permute-start.73) | collective-permute-done | bytes 1048608 | tf_op jit(solution)/shard_map/ppermute | solution.py:654
  552.0 13.1 %collective-permute-done.65 = bf16[128,4096]{1,0:T(8,128)(2,1)S(1)} collective-permute-done((bf16[128,4096]{1,0:T(8,128)(2,1)S(1)}, bf16[128,4096]{1,0:T(8,128)(2,1)S(1)}, u32[]{:S(2)}, u32[]{:S(2)}) %collective-permute-start.65) | collective-permute-done | bytes 1048608 | tf_op jit(solution)/shard_map/ppermute | solution.py:654
  569.8 11.4 %collective-permute-done.67 = bf16[64,4096]{1,0:T(8,128)(2,1)S(1)} collective-permute-done((bf16[64,4096]{1,0:T(8,128)(2,1)S(1)}, bf16[64,4096]{1,0:T(8,128)(2,1)S(1)}, u32[]{:S(2)}, u32[]{:S(2)}) %collective-permute-start.67) | collective-permute-done | bytes 524320 | tf_op jit(solution)/shard_map/ppermute | solution.py:705
  584.7 15.7 %collective-permute-done.68 = bf16[32,4096]{1,0:T(8,128)(2,1)S(1)} collective-permute-done((bf16[32,4096]{1,0:T(8,128)(2,1)S(1)}, bf16[32,4096]{1,0:T(8,128)(2,1)S(1)}, u32[]{:S(2)}, u32[]{:S(2)}) %collective-permute-start.68) | collective-permute-done | bytes 262176 | tf_op jit(solution)/shard_map/ppermute | solution.py:705
  600.5 11.1 %collective-permute-done.77 = bf16[128,1024]{1,0:T(8,128)(2,1)S(1)} collective-permute-done((bf16[128,1024]{1,0:T(8,128)(2,1)S(1)}, bf16[128,1024]{1,0:T(8,128)(2,1)S(1)}, u32[]{:S(2)}, u32[]{:S(2)}) %collective-permute-start.77) | collective-permute-done | bytes 262176 | tf_op jit(solution)/shard_map/ppermute | solution.py:705
  617.8 10.2 %collective-permute-done.78 = bf16[256,1024]{1,0:T(8,128)(2,1)S(1)} collective-permute-done((bf16[256,1024]{1,0:T(8,128)(2,1)S(1)}, bf16[256,1024]{1,0:T(8,128)(2,1)S(1)}, u32[]{:S(2)}, u32[]{:S(2)}) %collective-permute-start.78) | collective-permute-done | bytes 524320 | tf_op jit(solution)/shard_map/ppermute | solution.py:705
  629.9 9.3 %collective-permute-done.70 = bf16[64,4096]{1,0:T(8,128)(2,1)S(1)} collective-permute-done((bf16[64,4096]{1,0:T(8,128)(2,1)S(1)}, bf16[64,4096]{1,0:T(8,128)(2,1)S(1)}, u32[]{:S(2)}, u32[]{:S(2)}) %collective-permute-start.70) | collective-permute-done | bytes 524320 | tf_op jit(solution)/shard_map/ppermute | solution.py:705
  (362 shorter events, 227.1 us)
Async XLA Ops:
  9.3 40.2 %collective-permute-start.3 = (bf16[144,3072]{1,0:T(8,128)(2,1)S(1)}, bf16[144,3072]{1,0:T(8,128)(2,1)S(1)}, u32[]{:S(2)}, u32[]{:S(2)}) collective-permute-start(bf16[144,3072]{1,0:T(8,128)(2,1)S(1)} %fusion.7.refs_4_.refs_5_.refs_7_), channel_id=1, source_target_pairs={{0,16},{4,20},{8,24},{12,28},{16,0},{20,4},{24,8},{28,12},{1,17},{... | collective-permute-start | bytes 2654216 | tf_op jit(solution)/shard_map/ppermute | solution.py:654
  39.8 35.3 %collective-permute-start.26 = (bf16[128,4096]{1,0:T(8,128)(2,1)}, bf16[128,4096]{1,0:T(8,128)(2,1)}, u32[]{:S(2)}, u32[]{:S(2)}) collective-permute-start(bf16[128,4096]{1,0:T(8,128)(2,1)} %refs_4_.1), channel_id=1, source_target_pairs={{0,16},{4,20},{8,24},{12,28},{16,0},{20,4},{24,8},{28,12},{1,17},{... | collective-permute-start | bytes 3145736 | tf_op jit(solution)/shard_map/ppermute | solution.py:654
  64.9 28.4 %collective-permute-start.33 = (bf16[512,1024]{1,0:T(8,128)(2,1)}, bf16[512,1024]{1,0:T(8,128)(2,1)S(1)}, u32[]{:S(2)}, u32[]{:S(2)}) collective-permute-start(bf16[512,1024]{1,0:T(8,128)(2,1)} %refs_2_.3), channel_id=1, source_target_pairs={{0,16},{4,20},{8,24},{12,28},{16,0},{20,4},{24,8},{28,12},{1,17},{... | collective-permute-start | bytes 3145736 | tf_op jit(solution)/shard_map/ppermute | solution.py:654
  68.4 40.8 %collective-permute-start.31 = (bf16[512,1024]{1,0:T(8,128)(2,1)}, bf16[512,1024]{1,0:T(8,128)(2,1)S(1)}, u32[]{:S(2)}, u32[]{:S(2)}) collective-permute-start(bf16[512,1024]{1,0:T(8,128)(2,1)} %refs_2_.3), channel_id=1, source_target_pairs={{0,8},{4,12},{8,0},{12,4},{16,24},{20,28},{24,16},{28,20},{1,9},{5... | collective-permute-start | bytes 3145736 | tf_op jit(solution)/shard_map/ppermute | solution.py:654
  73.4 45.3 %collective-permute-start.9 = (bf16[480,1024]{1,0:T(8,128)(2,1)}, bf16[480,1024]{1,0:T(8,128)(2,1)}, u32[]{:S(2)}, u32[]{:S(2)}) collective-permute-start(bf16[480,1024]{1,0:T(8,128)(2,1)} %collective-permute-done.8.refs_1_), channel_id=1, source_target_pairs={{1,2},{2,3},{5,6},{6,7},{9,10},{10,11},{13,14},{14,15},{17,18},{18... | collective-permute-start | bytes 2949128 | tf_op jit(solution)/shard_map/ppermute | solution.py:742
  75.1 45.3 %collective-permute-start.11 = (bf16[480,1024]{1,0:T(8,128)(2,1)}, bf16[480,1024]{1,0:T(8,128)(2,1)}, u32[]{:S(2)}, u32[]{:S(2)}) collective-permute-start(bf16[480,1024]{1,0:T(8,128)(2,1)} %collective-permute-done.7.refs_0_), channel_id=1, source_target_pairs={{1,0},{2,1},{5,4},{6,5},{9,8},{10,9},{13,12},{14,13},{17,16},{18,1... | collective-permute-start | bytes 2949128 | tf_op jit(solution)/shard_map/ppermute | solution.py:743
  89.4 29.3 %collective-permute-start.5 = (bf16[144,3072]{1,0:T(8,128)(2,1)S(1)}, bf16[144,3072]{1,0:T(8,128)(2,1)S(1)}, u32[]{:S(2)}, u32[]{:S(2)}) collective-permute-start(bf16[144,3072]{1,0:T(8,128)(2,1)S(1)} %broadcast_select_fusion.2), channel_id=1, source_target_pairs={{0,8},{4,20},{8,0},{12,28},{16,24},{20,4},{24,16},{28,12},{1,9},{5... | collective-permute-start | bytes 2654216 | tf_op jit(solution)/shard_map/ppermute | solution.py:658
  93.3 30.0 %collective-permute-start.4 = (bf16[144,3072]{1,0:T(8,128)(2,1)S(1)}, bf16[144,3072]{1,0:T(8,128)(2,1)S(1)}, u32[]{:S(2)}, u32[]{:S(2)}) collective-permute-start(bf16[144,3072]{1,0:T(8,128)(2,1)S(1)} %collective-permute-done.3.refs_8_.refs_9_.refs_11_), channel_id=1, source_target_pairs={{0,4},{4,0},{8,12},{12,8},{16,20},{20,16},{24,28},{28,24},{1,5},{5... | collective-permute-start | bytes 2654216 | tf_op jit(solution)/shard_map/ppermute | solution.py:654
  124.0 50.6 %collective-permute-start.28 = (bf16[128,4096]{1,0:T(8,128)(2,1)S(1)}, bf16[128,4096]{1,0:T(8,128)(2,1)}, u32[]{:S(2)}, u32[]{:S(2)}) collective-permute-start(bf16[128,4096]{1,0:T(8,128)(2,1)S(1)} %broadcast_select_fusion.1), channel_id=1, source_target_pairs={{0,8},{4,20},{8,0},{12,28},{16,24},{20,4},{24,16},{28,12},{1,9},{5... | collective-permute-start | bytes 3145736 | tf_op jit(solution)/shard_map/ppermute | solution.py:658
  126.9 65.9 %collective-permute-start.23 = (bf16[128,4096]{1,0:T(8,128)(2,1)}, bf16[128,4096]{1,0:T(8,128)(2,1)}, u32[]{:S(2)}, u32[]{:S(2)}) collective-permute-start(bf16[128,4096]{1,0:T(8,128)(2,1)} %refs_4_.1), channel_id=1, source_target_pairs={{0,4},{4,0},{8,12},{12,8},{16,20},{20,16},{24,28},{28,24},{1,5},{5... | collective-permute-start | bytes 3145736 | tf_op jit(solution)/shard_map/ppermute | solution.py:654
  127.0 65.9 %collective-permute-start.27 = (bf16[128,4096]{1,0:T(8,128)(2,1)}, bf16[128,4096]{1,0:T(8,128)(2,1)}, u32[]{:S(2)}, u32[]{:S(2)}) collective-permute-start(bf16[128,4096]{1,0:T(8,128)(2,1)} %collective-permute-done.26.refs_6_.refs_8_), channel_id=1, source_target_pairs={{0,4},{4,0},{8,12},{12,8},{16,20},{20,16},{24,28},{28,24},{1,5},{5... | collective-permute-start | bytes 3145736 | tf_op jit(solution)/shard_map/ppermute | solution.py:654
  127.5 68.6 %collective-permute-start.25 = (bf16[128,4096]{1,0:T(8,128)(2,1)}, bf16[128,4096]{1,0:T(8,128)(2,1)}, u32[]{:S(2)}, u32[]{:S(2)}) collective-permute-start(bf16[128,4096]{1,0:T(8,128)(2,1)} %collective-permute-done.24.refs_4_.refs_6_), channel_id=1, source_target_pairs={{0,4},{4,0},{8,12},{12,8},{16,20},{20,16},{24,28},{28,24},{1,5},{5... | collective-permute-start | bytes 3145736 | tf_op jit(solution)/shard_map/ppermute | solution.py:654
  146.7 50.7 %collective-permute-start.35 = (bf16[512,1024]{1,0:T(8,128)(2,1)}, bf16[512,1024]{1,0:T(8,128)(2,1)}, u32[]{:S(2)}, u32[]{:S(2)}) collective-permute-start(bf16[512,1024]{1,0:T(8,128)(2,1)} %broadcast_select_fusion), channel_id=1, source_target_pairs={{0,8},{4,20},{8,0},{12,28},{16,24},{20,4},{24,16},{28,12},{1,9},{5... | collective-permute-start | bytes 3145736 | tf_op jit(solution)/shard_map/ppermute | solution.py:658
  174.6 50.9 %collective-permute-start.29 = (bf16[128,4096]{1,0:T(8,128)(2,1)}, bf16[128,4096]{1,0:T(8,128)(2,1)}, u32[]{:S(2)}, u32[]{:S(2)}) collective-permute-start(bf16[128,4096]{1,0:T(8,128)(2,1)} %collective-permute-done.28.refs_8_.refs_10_), channel_id=1, source_target_pairs={{0,4},{4,0},{8,12},{12,8},{16,20},{20,16},{24,28},{28,24},{1,5},{5... | collective-permute-start | bytes 3145736 | tf_op jit(solution)/shard_map/ppermute | solution.py:654
  197.3 41.3 %collective-permute-start.30 = (bf16[512,1024]{1,0:T(8,128)(2,1)}, bf16[512,1024]{1,0:T(8,128)(2,1)}, u32[]{:S(2)}, u32[]{:S(2)}) collective-permute-start(bf16[512,1024]{1,0:T(8,128)(2,1)} %refs_2_.3), channel_id=1, source_target_pairs={{0,4},{4,0},{8,12},{12,8},{16,20},{20,16},{24,28},{28,24},{1,5},{5... | collective-permute-start | bytes 3145736 | tf_op jit(solution)/shard_map/ppermute | solution.py:654
  203.9 34.8 %collective-permute-start.34 = (bf16[512,1024]{1,0:T(8,128)(2,1)S(1)}, bf16[512,1024]{1,0:T(8,128)(2,1)}, u32[]{:S(2)}, u32[]{:S(2)}) collective-permute-start(bf16[512,1024]{1,0:T(8,128)(2,1)S(1)} %copy-done.10), channel_id=1, source_target_pairs={{0,4},{4,0},{8,12},{12,8},{16,20},{20,16},{24,28},{28,24},{1,5},{5... | collective-permute-start | bytes 3145736 | tf_op jit(solution)/shard_map/ppermute | solution.py:654
  288.0 123.2 %collective-permute-start.55 = (bf16[4,128,1024]{2,1,0:T(8,128)(2,1)}, bf16[4,128,1024]{2,1,0:T(8,128)(2,1)S(1)}, u32[]{:S(2)}, u32[]{:S(2)}) collective-permute-start(bf16[4,128,1024]{2,1,0:T(8,128)(2,1)} %outer_mix1.1), channel_id=1, source_target_pairs={{0,4},{4,0},{8,12},{12,8},{16,20},{20,16},{24,28},{28,24},{1,5},{5... | collective-permute-start | bytes 3145736 | tf_op jit(solution)/shard_map/ppermute | solution.py:654
  294.9 167.9 %collective-permute-start.71 = (bf16[4,512,1024]{2,1,0:T(8,128)(2,1)}, bf16[4,512,1024]{2,1,0:T(8,128)(2,1)}, u32[]{:S(2)}, u32[]{:S(2)}) collective-permute-start(bf16[4,512,1024]{2,1,0:T(8,128)(2,1)} %outer_rows1.1), channel_id=1, source_target_pairs={{0,4},{4,0},{8,12},{12,8},{16,20},{20,16},{24,28},{28,24},{1,5},{5... | collective-permute-start | bytes 12582920 | tf_op jit(solution)/shard_map/ppermute | solution.py:654
  332.0 50.6 %collective-permute-start.41 = (bf16[480,768]{1,0:T(8,128)(2,1)}, bf16[480,768]{1,0:T(8,128)(2,1)}, u32[]{:S(2)}, u32[]{:S(2)}) collective-permute-start(bf16[480,768]{1,0:T(8,128)(2,1)} %get-tuple-element.67.refs_6_), channel_id=1, source_target_pairs={{0,2},{1,3},{2,0},{3,1},{4,6},{5,7},{6,4},{7,5},{8,10},{9,11},{10,... | collective-permute-start | bytes 2211848 | tf_op jit(solution)/shard_map/ppermute | solution.py:709
  333.8 48.8 %collective-permute-start.42 = (bf16[480,768]{1,0:T(8,128)(2,1)S(1)}, bf16[480,768]{1,0:T(8,128)(2,1)}, u32[]{:S(2)}, u32[]{:S(2)}) collective-permute-start(bf16[480,768]{1,0:T(8,128)(2,1)S(1)} %copy-done.12), channel_id=1, source_target_pairs={{0,3},{1,0},{2,1},{3,2},{4,7},{5,4},{6,5},{7,6},{8,11},{9,8},{10,9... | collective-permute-start | bytes 2211848 | tf_op jit(solution)/shard_map/ppermute | solution.py:709
  352.3 122.9 %collective-permute-start.63 = (bf16[4,128,4096]{2,1,0:T(8,128)(2,1)}, bf16[4,128,4096]{2,1,0:T(8,128)(2,1)}, u32[]{:S(2)}, u32[]{:S(2)}) collective-permute-start(bf16[4,128,4096]{2,1,0:T(8,128)(2,1)} %outer_wide1.1), channel_id=1, source_target_pairs={{0,4},{4,0},{8,12},{12,8},{16,20},{20,16},{24,28},{28,24},{1,5},{5... | collective-permute-start | bytes 12582920 | tf_op jit(solution)/shard_map/ppermute | solution.py:654
  410.4 36.6 %collective-permute-start.49 = (bf16[128,768]{1,0:T(8,128)(2,1)}, bf16[128,768]{1,0:T(8,128)(2,1)S(1)}, u32[]{:S(2)}, u32[]{:S(2)}) collective-permute-start(bf16[128,768]{1,0:T(8,128)(2,1)} %slice_bitcast_fusion.13), channel_id=1, source_target_pairs={{0,8},{4,20},{8,0},{12,28},{16,24},{20,4},{24,16},{28,12},{1,9},{5... | collective-permute-start | bytes 589832 | tf_op jit(solution)/shard_map/ppermute | solution.py:658
  458.2 31.7 %collective-permute-start.54 = (bf16[128,768]{1,0:T(8,128)(2,1)}, bf16[128,768]{1,0:T(8,128)(2,1)}, u32[]{:S(2)}, u32[]{:S(2)}) collective-permute-start(bf16[128,768]{1,0:T(8,128)(2,1)} %fusion.14), channel_id=1, source_target_pairs={{0,3},{1,0},{2,1},{3,2},{4,7},{5,4},{6,5},{7,6},{8,11},{9,8},{10,9... | collective-permute-start | bytes 589832 | tf_op jit(solution)/shard_map/ppermute | solution.py:709
  461.7 42.5 %collective-permute-start.53 = (bf16[128,768]{1,0:T(8,128)(2,1)}, bf16[128,768]{1,0:T(8,128)(2,1)}, u32[]{:S(2)}, u32[]{:S(2)}) collective-permute-start(bf16[128,768]{1,0:T(8,128)(2,1)} %fusion.14), channel_id=1, source_target_pairs={{0,2},{1,3},{2,0},{3,1},{4,6},{5,7},{6,4},{7,5},{8,10},{9,11},{10,... | collective-permute-start | bytes 589832 | tf_op jit(solution)/shard_map/ppermute | solution.py:709
  461.7 44.6 %collective-permute-start.52 = (bf16[128,768]{1,0:T(8,128)(2,1)}, bf16[128,768]{1,0:T(8,128)(2,1)}, u32[]{:S(2)}, u32[]{:S(2)}) collective-permute-start(bf16[128,768]{1,0:T(8,128)(2,1)} %fusion.14), channel_id=1, source_target_pairs={{0,1},{1,2},{2,3},{3,0},{4,5},{5,6},{6,7},{7,4},{8,9},{9,10},{10,1... | collective-permute-start | bytes 589832 | tf_op jit(solution)/shard_map/ppermute | solution.py:709
  475.3 44.9 %collective-permute-start.72 = (bf16[512,1024]{1,0:T(8,128)(2,1)}, bf16[512,1024]{1,0:T(8,128)(2,1)}, u32[]{:S(2)}, u32[]{:S(2)}) collective-permute-start(bf16[512,1024]{1,0:T(8,128)(2,1)} %slice_bitcast_fusion.1), channel_id=1, source_target_pairs={{0,8},{4,20},{8,0},{12,28},{16,24},{20,4},{24,16},{28,12},{1,9},{5... | collective-permute-start | bytes 3145736 | tf_op jit(solution)/shard_map/ppermute | solution.py:658
  488.3 37.0 %collective-permute-start.64 = (bf16[128,4096]{1,0:T(8,128)(2,1)}, bf16[128,4096]{1,0:T(8,128)(2,1)}, u32[]{:S(2)}, u32[]{:S(2)}) collective-permute-start(bf16[128,4096]{1,0:T(8,128)(2,1)} %slice_bitcast_fusion.5), channel_id=1, source_target_pairs={{0,8},{4,20},{8,0},{12,28},{16,24},{20,4},{24,16},{28,12},{1,9},{5... | collective-permute-start | bytes 3145736 | tf_op jit(solution)/shard_map/ppermute | solution.py:658
  490.0 28.2 %collective-permute-start.60 = (bf16[32,1024]{1,0:T(8,128)(2,1)S(1)}, bf16[32,1024]{1,0:T(8,128)(2,1)S(1)}, u32[]{:S(2)}, u32[]{:S(2)}) collective-permute-start(bf16[32,1024]{1,0:T(8,128)(2,1)S(1)} %select_convert_fusion.5), channel_id=1, source_target_pairs={{0,2},{1,3},{2,0},{3,1},{4,6},{5,7},{6,4},{7,5},{8,10},{9,11},{10,... | collective-permute-start | bytes 196616 | tf_op jit(solution)/shard_map/ppermute | solution.py:705
  527.1 37.9 %collective-permute-start.65 = (bf16[128,4096]{1,0:T(8,128)(2,1)S(1)}, bf16[128,4096]{1,0:T(8,128)(2,1)S(1)}, u32[]{:S(2)}, u32[]{:S(2)}) collective-permute-start(bf16[128,4096]{1,0:T(8,128)(2,1)S(1)} %get-tuple-element.81), channel_id=1, source_target_pairs={{0,8},{4,12},{8,0},{12,4},{16,24},{20,28},{24,16},{28,20},{1,9},{5... | collective-permute-start | bytes 3145736 | tf_op jit(solution)/shard_map/ppermute | solution.py:654
  528.0 38.1 %collective-permute-start.66 = (bf16[128,4096]{1,0:T(8,128)(2,1)S(1)}, bf16[128,4096]{1,0:T(8,128)(2,1)S(1)}, u32[]{:S(2)}, u32[]{:S(2)}) collective-permute-start(bf16[128,4096]{1,0:T(8,128)(2,1)S(1)} %get-tuple-element.82), channel_id=1, source_target_pairs={{0,16},{4,20},{8,24},{12,28},{16,0},{20,4},{24,8},{28,12},{1,17},{... | collective-permute-start | bytes 3145736 | tf_op jit(solution)/shard_map/ppermute | solution.py:654
  530.8 51.3 %collective-permute-start.62 = (bf16[64,1024]{1,0:T(8,128)(2,1)S(1)}, bf16[64,1024]{1,0:T(8,128)(2,1)S(1)}, u32[]{:S(2)}, u32[]{:S(2)}) collective-permute-start(bf16[64,1024]{1,0:T(8,128)(2,1)S(1)} %pad_maximum_fusion.2), channel_id=1, source_target_pairs={{0,1},{1,0},{2,3},{3,2},{4,5},{5,4},{6,7},{7,6},{8,9},{9,8},{10,11... | collective-permute-start | bytes 393224 | tf_op jit(solution)/shard_map/ppermute | solution.py:705
  582.3 29.3 %collective-permute-start.77 = (bf16[128,1024]{1,0:T(8,128)(2,1)S(1)}, bf16[128,1024]{1,0:T(8,128)(2,1)S(1)}, u32[]{:S(2)}, u32[]{:S(2)}) collective-permute-start(bf16[128,1024]{1,0:T(8,128)(2,1)S(1)} %add_convert_fusion), channel_id=1, source_target_pairs={{0,2},{1,3},{2,0},{3,1},{4,6},{5,7},{6,4},{7,5},{8,10},{9,11},{10,... | collective-permute-start | bytes 786440 | tf_op jit(solution)/shard_map/ppermute | solution.py:705
  (83 other events, 1476.9 us)
